TPU v7x, 32 devices: a whole 2x2x4 slice. The times are simulated.
32 devices in a mesh: clips: 2 (over y), pix: 4 (over z), pair: 2 (over x), dir: 2 (over core).
Axes of the slice: x: 2, y: 2, z: 4, core: 2. Of those that a mesh axis runs over, the one named last changes fastest.
Arguments:
- features: bfloat16 [4, 2, 1920, 128], P(('clips', 'pair'), 'dir', 'pix'), parts along dimension 0, may hold values from -6 to 6
Outputs:
- flow: float32 [4, 2, 2, 1920], P(('clips', 'pair'), 'dir', None, 'pix'), parts along dimension 0
- matched: bfloat16 [4, 2, 1920, 128], P(('clips', 'pair'), 'dir', 'pix'), parts along dimension 0
There are 2 independent parts, one for each index of `clips`. A program takes and returns all parts, laid end to end along the dimension named above; each array names one. Nothing has to cross between parts.
All inputs are finite; a program needn't handle non-finite values.
Results may differ from a plain program's by a relative error of at most 0.0065.
Values may be sent and summed in bfloat16 or wider, within the bound.
No kernel may reach another device: no remote copies, remote signals or barrier semaphores. Data moves between devices by JAX's collectives and lax.ppermute only.
A program may use at most 64 MiB of HBM per device.

v0:
```python
import jax
import jax.numpy as jnp
from jax import lax
from jax.sharding import PartitionSpec as P

C = 128
W = 120


def from_partner(array, axis, bit):
    return lax.ppermute(array, axis, [(i, i ^ 1 << bit) for i in range(lax.axis_size(axis))])


def positions(index):
    return ((index % W).astype(jnp.float32) / W, (index // W).astype(jnp.float32) / W)


def fold_part(carry, queries, keys, start):
    top, total, sum_x, sum_y, acc = carry
    scores = lax.dot_general(
        queries, keys, (((1,), (1,)), ((), ())), preferred_element_type=jnp.float32
    ) * C ** (-0.5)
    posx, posy = positions(start + jnp.arange(keys.shape[0], dtype=jnp.int32))
    new_top = jnp.maximum(top, jnp.max(scores, axis=1))
    fade = jnp.exp(top - new_top)
    weights = jnp.exp(scores - new_top[:, None])
    total = total * fade + jnp.sum(weights, axis=1)
    sum_x = sum_x * fade + jnp.sum(weights * posx[None, :], axis=1)
    sum_y = sum_y * fade + jnp.sum(weights * posy[None, :], axis=1)
    acc = acc * fade[:, None] + jnp.dot(
        weights.astype(jnp.bfloat16), keys, preferred_element_type=jnp.float32
    )
    return (new_top, total, sum_x, sum_y, acc)


def make_step(queries, carry, piece):
    keys = piece.reshape(-1, piece.shape[-1])
    length = keys.shape[0]
    width = length
    while width > 1536 and width % 2 == 0:
        width = width // 2
    blocks = keys.reshape(length // width, width, keys.shape[1])

    def inner(state, item):
        return (fold_part(state, queries, item[0], item[1] * width), None)

    result, unused = lax.scan(inner, carry, (blocks, jnp.arange(length // width, dtype=jnp.int32)))
    return result


def finish(carry, first_row):
    top, total, sum_x, sum_y, acc = carry
    own_x, own_y = positions(first_row + jnp.arange(total.shape[0], dtype=jnp.int32))
    flow = jnp.stack([sum_x / total - own_x, sum_y / total - own_y])
    matched = (acc / total[:, None]).astype(jnp.bfloat16)
    return (flow, matched)


def body(features):
    rows_here = features.shape[2]
    chans = features.shape[3]
    first_row = lax.axis_index("pix") * rows_here
    init = (
        jnp.full((rows_here,), -jnp.inf, jnp.float32),
        jnp.zeros((rows_here,), jnp.float32),
        jnp.zeros((rows_here,), jnp.float32),
        jnp.zeros((rows_here,), jnp.float32),
        jnp.zeros((rows_here, chans), jnp.float32),
    )
    foreign = from_partner(features, "dir", 0)
    carry = make_step(
        foreign.reshape(rows_here, chans), init, lax.all_gather(features, "pix", axis=2, tiled=True)
    )
    other_flow, other_matched = finish(carry, first_row)
    flow, wide_matched = (
        from_partner(other_flow.astype(jnp.bfloat16), "dir", 0).astype(other_flow.dtype),
        from_partner(other_matched.astype(jnp.float32).astype(jnp.bfloat16), "dir", 0).astype(
            jnp.float32
        ),
    )
    matched = wide_matched.astype(jnp.bfloat16)
    return (flow.reshape(1, 1, 2, rows_here), matched.reshape(1, 1, rows_here, chans))


def solution(mesh):
    placed = (P(("clips", "pair"), "dir", "pix", None),)
    return jax.shard_map(
        body,
        mesh=mesh,
        in_specs=placed,
        out_specs=(
            P(("clips", "pair"), "dir", None, "pix"),
            P(("clips", "pair"), "dir", "pix", None),
        ),
        check_vma=False,
    )
```

profile of v0, /device:TPU:0, one launch (start us, length us, event | category | flops | bytes accessed | tf_op | source)
XLA Modules:
  0.0 27.1 jit_solution(562660175791292851)
XLA Ops:
  0.6 0.6 %collective-permute-start = (bf16[1,1,480,128]{3,2,1,0:T(8,128)(2,1)}, bf16[1,1,480,128]{3,2,1,0:T(8,128)(2,1)S(1)}, u32[]{:S(2)}, u32[]{:S(2)}) collective-permute-start(bf16[1,1,480,128]{3,2,1,0:T(8,128)(2,1)} %param.3), channel_id=1, source_target_pairs={{0,1},{1,0},{2,3},{3,2},{4,5},{5,4},{6,7},{7,6},{8,9},{9,8},{10,11... | collective-permute-start | bytes 368648 | tf_op jit(solution)/shard_map/ppermute | solution.py:11
  1.2 17.3 %all_gather.3 = bf16[1,1,1920,128]{3,2,1,0:T(8,128)(2,1)S(1)} all-gather(bf16[1,1,480,128]{3,2,1,0:T(8,128)(2,1)} %param.3), channel_id=1, replica_groups=mesh['clips'=2,'pix'=4,'pair'=2,'dir'=2] {'pix'}, dimensions={2}, use_global_device_ids=true | all-gather | bytes 614400 | tf_op jit(solution)/shard_map/all_gather | solution.py:72
  18.5 0.0 collective-permute-done
  18.5 6.0 %while.21 = (s32[]{:T(128)}, f32[480]{0:T(512)S(1)}, f32[480]{0:T(512)S(1)}, f32[480]{0:T(512)S(1)}, f32[480]{0:T(512)S(1)}, /*index=5*/f32[480,128]{1,0:T(8,128...) while((s32[]{:T(128)}, f32[480]{0:T(512)S(1)}, ...), condition=%wide.region_5.6_spmd.clone, body=%wide.region_0.5_spmd.clone.sunk | while | flops 241664160 | bytes 6822190 | solution.py:47
  18.5 0.6 %dynamic_slice.31 = s32[1]{0:T(128)} dynamic-slice(s32[2]{0:T(128)S(1)} %get-tuple-element.295, s32[]{:T(128)S(6)} %copy.9), dynamic_slice_sizes={1} | dynamic-slice | bytes 12 | tf_op jit(solution)/shard_map/while/body/jit(dynamic_index_in_dim)/dynamic_slice | solution.py:47
  19.8 0.5 %multiply_reduce_fusion.5 = (f32[480]{0:T(512)S(1)}, f32[960,480]{1,0:T(8,128)S(1)}) fusion(bf16[480,128]{1,0:T(8,128)(2,1)S(1)} %get-tuple-element.294, bf16[2,960,128]{2,1,0:T(8,128)(2,1)S(1)} %get-tuple-element.293, s32[]{:T(128)S(6)} %copy.9), kind=kOutput, calls=%fused_computation.3.clone.1 | convolution fusion | flops 118885920 | bytes 2213764 | tf_op jit(solution)/shard_map/while/body/eval_jaxpr/dot_general | solution.py:20
  20.3 0.6 %multiply_reduce_fusion.6 = (f32[480]{0:T(512)S(1)}, f32[480]{0:T(512)S(1)}, f32[480]{0:T(512)S(1)}) fusion(f32[960]{0:T(1024)S(1)} %get-tuple-element.253, f32[480]{0:T(512)S(1)} %select_maximum_fusion.2, f32[960,480]{1,0:T(8,128)S(1)} %get-tuple-element.254, f32[960]{0:T(1024)S(1)} %get-tuple-element.255), kind=kLoop, calls=%fused_computation.clone.1 | loop fusion | flops 3224160 | bytes 1858560 | tf_op jit(solution)/shard_map/while/body/eval_jaxpr/reduce_sum | solution.py:29
  21.0 0.5 %convolution_add_fusion.2 = f32[480,128]{1,0:T(8,128)S(1)} fusion(f32[960,480]{1,0:T(8,128)S(1)} %get-tuple-element.254, f32[480]{0:T(512)S(1)} %select_maximum_fusion.2, f32[480,128]{1,0:T(8,128)S(1)} %get-tuple-element.280, bf16[2,960,128]{2,1,0:T(8,128)(2,1)S(1)} %get-tuple-element.293, s32[]{:T(128)S(6)} %copy.9, f32[480]{0:T(512)S(1)} %get-tuple-element.258, ...), kind=kOutput, calls=%fused_computation.4.clone.1 | convolution fusion | flops 119531520 | bytes 2707461 | tf_op jit(solution)/shard_map/while/body/eval_jaxpr/dot_general | solution.py:30
  21.5 0.6 %dynamic_slice.31 = s32[1]{0:T(128)} dynamic-slice(s32[2]{0:T(128)S(1)} %get-tuple-element.295, s32[]{:T(128)S(6)} %copy.9), dynamic_slice_sizes={1} | dynamic-slice | bytes 12 | tf_op jit(solution)/shard_map/while/body/jit(dynamic_index_in_dim)/dynamic_slice | solution.py:47
  22.8 0.5 %multiply_reduce_fusion.5 = (f32[480]{0:T(512)S(1)}, f32[960,480]{1,0:T(8,128)S(1)}) fusion(bf16[480,128]{1,0:T(8,128)(2,1)S(1)} %get-tuple-element.294, bf16[2,960,128]{2,1,0:T(8,128)(2,1)S(1)} %get-tuple-element.293, s32[]{:T(128)S(6)} %copy.9), kind=kOutput, calls=%fused_computation.3.clone.1 | convolution fusion | flops 118885920 | bytes 2213764 | tf_op jit(solution)/shard_map/while/body/eval_jaxpr/dot_general | solution.py:20
  23.3 0.6 %multiply_reduce_fusion.6 = (f32[480]{0:T(512)S(1)}, f32[480]{0:T(512)S(1)}, f32[480]{0:T(512)S(1)}) fusion(f32[960]{0:T(1024)S(1)} %get-tuple-element.253, f32[480]{0:T(512)S(1)} %select_maximum_fusion.2, f32[960,480]{1,0:T(8,128)S(1)} %get-tuple-element.254, f32[960]{0:T(1024)S(1)} %get-tuple-element.255), kind=kLoop, calls=%fused_computation.clone.1 | loop fusion | flops 3224160 | bytes 1858560 | tf_op jit(solution)/shard_map/while/body/eval_jaxpr/reduce_sum | solution.py:29
  24.0 0.5 %convolution_add_fusion.2 = f32[480,128]{1,0:T(8,128)S(1)} fusion(f32[960,480]{1,0:T(8,128)S(1)} %get-tuple-element.254, f32[480]{0:T(512)S(1)} %select_maximum_fusion.2, f32[480,128]{1,0:T(8,128)S(1)} %get-tuple-element.280, bf16[2,960,128]{2,1,0:T(8,128)(2,1)S(1)} %get-tuple-element.293, s32[]{:T(128)S(6)} %copy.9, f32[480]{0:T(512)S(1)} %get-tuple-element.258, ...), kind=kOutput, calls=%fused_computation.4.clone.1 | convolution fusion | flops 119531520 | bytes 2707461 | tf_op jit(solution)/shard_map/while/body/eval_jaxpr/dot_general | solution.py:30
  24.6 0.1 collective-permute-start.1
  24.7 0.1 divide_convert_fusion
  24.8 0.6 %collective-permute-start.2 = (bf16[480,128]{1,0:T(8,128)(2,1)S(1)}, bf16[480,128]{1,0:T(8,128)(2,1)S(1)}, u32[]{:S(2)}, u32[]{:S(2)}) collective-permute-start(bf16[480,128]{1,0:T(8,128)(2,1)S(1)} %divide_convert_fusion), channel_id=1, source_target_pairs={{0,1},{1,0},{2,3},{3,2},{4,5},{5,4},{6,7},{7,6},{8,9},{9,8},{10,11... | collective-permute-start | bytes 368648 | tf_op jit(solution)/shard_map/ppermute | solution.py:11
  25.4 0.4 %collective-permute-done.1 = bf16[2,480]{1,0:T(2,128)(2,1)S(1)} collective-permute-done((bf16[2,480]{1,0:T(2,128)(2,1)S(1)}, bf16[2,480]{1,0:T(2,128)(2,1)S(1)}, u32[]{:S(2)}, u32[]{:S(2)}) %collective-permute-start.1) | collective-permute-done | bytes 1952 | tf_op jit(solution)/shard_map/ppermute | solution.py:11
  25.8 0.6 %bitcast_convert_fusion = f32[1,1,2,480]{3,2,1,0:T(2,128)} fusion(bf16[2,480]{1,0:T(2,128)(2,1)S(1)} %collective-permute-done.1), kind=kLoop, calls=%fused_computation.45 | loop fusion | flops 960 | bytes 5760 | tf_op jit(solution)/shard_map/reshape | solution.py:82
  26.4 0.0 collective-permute-done.2
  26.4 0.6 %copy.22 = bf16[1,1,480,128]{3,2,1,0:T(8,128)(2,1)} copy(bf16[1,1,480,128]{3,2,1,0:T(8,128)(2,1)S(1)} %bitcast.25) | data formatting | bytes 245760
  (20 shorter events, 0.2 us)
Async XLA Ops:
  0.6 17.9 %collective-permute-start = (bf16[1,1,480,128]{3,2,1,0:T(8,128)(2,1)}, bf16[1,1,480,128]{3,2,1,0:T(8,128)(2,1)S(1)}, u32[]{:S(2)}, u32[]{:S(2)}) collective-permute-start(bf16[1,1,480,128]{3,2,1,0:T(8,128)(2,1)} %param.3), channel_id=1, source_target_pairs={{0,1},{1,0},{2,3},{3,2},{4,5},{5,4},{6,7},{7,6},{8,9},{9,8},{10,11... | collective-permute-start | bytes 368648 | tf_op jit(solution)/shard_map/ppermute | solution.py:11
  24.6 1.2 %collective-permute-start.1 = (bf16[2,480]{1,0:T(2,128)(2,1)S(1)}, bf16[2,480]{1,0:T(2,128)(2,1)S(1)}, u32[]{:S(2)}, u32[]{:S(2)}) collective-permute-start(bf16[2,480]{1,0:T(2,128)(2,1)S(1)} %pad_maximum_fusion), channel_id=1, source_target_pairs={{0,1},{1,0},{2,3},{3,2},{4,5},{5,4},{6,7},{7,6},{8,9},{9,8},{10,11... | collective-permute-start | bytes 5768 | tf_op jit(solution)/shard_map/ppermute | solution.py:11
  24.8 1.6 %collective-permute-start.2 = (bf16[480,128]{1,0:T(8,128)(2,1)S(1)}, bf16[480,128]{1,0:T(8,128)(2,1)S(1)}, u32[]{:S(2)}, u32[]{:S(2)}) collective-permute-start(bf16[480,128]{1,0:T(8,128)(2,1)S(1)} %divide_convert_fusion), channel_id=1, source_target_pairs={{0,1},{1,0},{2,3},{3,2},{4,5},{5,4},{6,7},{7,6},{8,9},{9,8},{10,11... | collective-permute-start | bytes 368648 | tf_op jit(solution)/shard_map/ppermute | solution.py:11
where the time goes:
time: 27.3 us; the launch traced here: 27.1 us
  blocking collectives  17.3 us (63%)
  other arithmetic  2.18 us (8%)
  matrix products  2.06 us (8%)
  local copies, waits for them, and re-layouts  1.84 us (7%)
  loops' own time  1.38 us (5%)
  starting transfers between devices  1.19 us (4%)
  between operations  0.68 us (2%)
  waiting for transfers between devices  0.45 us (2%)
    all_gather x1, blocking collectives, body(): lax.all_gather(features, 'pix', axis=2, tiled=True)  17.3 us
    another operation x1, loops' own time, make_step(): lax.scan(inner, carry, (blocks, jnp.arange(length // width, dtype=jnp.int...  1.38 us
    reduce_sum x2, other arithmetic, fold_part(): sum_y = sum_y * fade + jnp.sum(weights * posy[None, :], axis=1)  1.29 us
    ppermute x3, starting transfers between devices, from_partner(): lax.ppermute(array, axis, [(i, i ^ 1 << bit) for i in range(lax.axis_size...  1.19 us
    dynamic_slice x2, local copies, waits for them, and re-layouts, make_step(): lax.scan(inner, carry, (blocks, jnp.arange(length // width, dtype=jnp.int...  1.17 us
    dot_general x2, matrix products, fold_part(): jnp.dot(weights.astype(jnp.bfloat16), keys, preferred_element_type=jnp.fl...  1.07 us
    dot_general x2, matrix products, fold_part(): lax.dot_general(queries, keys, (((1,), (1,)), ((), ())), preferred_elemen...  1 us
    unnamed x1, local copies, waits for them, and re-layouts  0.65 us
  transfers between devices with their start and end apart: 3, of which 1 were waited for; matrix products, arithmetic and copies ran while one was open for 3% of the time, Pallas kernels for 0%

commit v1 on v0

v1 whole, which is shorter than its diff:
```python
import functools
import math

import jax
import jax.numpy as jnp
from jax import lax
from jax.experimental import pallas as pl
from jax.experimental.pallas import tpu as pltpu
from jax.sharding import PartitionSpec as P

W = 120
FORWARD = 0.0
VMEM = pl.BlockSpec(memory_space=pltpu.VMEM)


def hop(array, shift, cross):
    pix, frames = lax.axis_size("pix"), lax.axis_size("dir")
    flip = 1 if cross else 0
    pairs = [
        (z * frames + d, (z ^ shift) * frames + (d ^ flip)) for z in range(pix) for d in range(frames)
    ]
    return lax.ppermute(array, ("pix", "dir"), pairs)


def local_positions(rows, chans):
    column = lax.broadcasted_iota(jnp.int32, (rows, chans), 1)
    index = lax.broadcasted_iota(jnp.int32, (rows, chans), 0).astype(jnp.float32)
    row = jnp.floor((index + 0.5) * (1.0 / W))
    place = index - row * W
    values = jnp.where(column == 0, place, jnp.where(column == 1, row, 1.0))
    return jnp.where(column < 3, values, 0.0).astype(jnp.bfloat16)


def fold_kernel(shifts, counts, first, last, rows_here, *refs):
    refs = list(refs)
    q_ref = refs.pop(0)
    key_refs = [[refs.pop(0) for _ in range(n)] for n in counts]
    if not first:
        top_in, acc_in, pos_in = refs.pop(0), refs.pop(0), refs.pop(0)
        pos = pos_in[...]
    else:
        pos = local_positions(rows_here, q_ref.shape[1])
    queries = q_ref[...]
    chans = queries.shape[1]
    scale = chans ** (-0.5) * math.log2(math.e)
    here = lax.axis_index("pix")
    column = lax.broadcasted_iota(jnp.int32, (1, chans), 1)
    keys, values = [], []
    for shift, block in zip(shifts, key_refs):
        part = jnp.concatenate([ref[...] for ref in block], axis=0) if len(block) > 1 else block[0][...]
        start_row = (here ^ shift) * (rows_here // W)
        offset = jnp.where(column == 1, start_row, 0).astype(jnp.float32).astype(jnp.bfloat16)
        keys.append(part)
        values.append(jnp.concatenate([part, pos + offset], axis=1))
    keys = jnp.concatenate(keys, axis=0) if len(keys) > 1 else keys[0]
    values = jnp.concatenate(values, axis=0) if len(values) > 1 else values[0]
    scores = lax.dot_general(queries, keys, (((1,), (1,)), ((), ())), preferred_element_type=jnp.float32)
    top = jnp.max(scores, axis=1, keepdims=True)
    if not first:
        old = top_in[...]
        top = jnp.maximum(old[:, :1], top)
    weights = jnp.exp2((scores - top) * scale).astype(jnp.bfloat16)
    acc = jnp.dot(weights, values, preferred_element_type=jnp.float32)
    if not first:
        acc = acc + acc_in[...] * jnp.exp2((old[:, :1] - top) * scale)
    if not last:
        top_out, acc_out = refs.pop(0), refs.pop(0)
        top_out[...] = jnp.broadcast_to(top, top_out.shape)
        acc_out[...] = acc
        if first:
            refs.pop(0)[...] = pos
        return
    flow_ref, matched_ref = refs
    inverse = 1.0 / acc[:, chans + 2 : chans + 3]
    matched_ref[...] = (acc[:, :chans] * inverse).astype(jnp.bfloat16)
    sums = jnp.transpose(acc[:, chans:] * inverse)[:2, :]
    index = (here * rows_here + lax.broadcasted_iota(jnp.int32, (1, rows_here), 1)).astype(jnp.float32)
    own_row = jnp.floor((index + 0.5) * (1.0 / W))
    own_place = index - own_row * W
    flow_ref[...] = (sums - jnp.concatenate([own_place, own_row], axis=0)) * (1.0 / W)


def fold(queries, blocks, carry, last):
    rows, chans = queries.shape
    shifts = [shift for shift, _ in blocks]
    counts = [len(parts) for _, parts in blocks]
    first = carry is None
    if last:
        shapes = ((2, rows), jnp.float32), ((rows, chans), jnp.bfloat16)
    else:
        shapes = ((rows, chans), jnp.float32), ((rows, 2 * chans), jnp.float32)
        if first:
            shapes += (((rows, chans), jnp.bfloat16),)
    operands = [queries] + [part for _, parts in blocks for part in parts] + list(carry or ())
    keys = sum(part.shape[0] for _, parts in blocks for part in parts)
    outs = pl.pallas_call(
        functools.partial(fold_kernel, shifts, counts, first, last, rows),
        out_shape=[jax.ShapeDtypeStruct(shape, kind) for shape, kind in shapes],
        in_specs=[VMEM] * len(operands),
        out_specs=[VMEM] * len(shapes),
        compiler_params=pltpu.CompilerParams(vmem_limit_bytes=24 * 1024 * 1024),
        cost_estimate=pl.CostEstimate(
            flops=6 * rows * keys * chans, bytes_accessed=2 * keys * chans, transcendentals=rows * keys
        ),
    )(*operands)
    if last:
        return outs
    return (outs[0], outs[1], outs[2] if first else carry[2])


def body(features):
    rows, chans = features.shape[2:]
    pix = lax.axis_size("pix")
    cut = int(rows * FORWARD) // 32 * 32
    own = features.reshape(rows, chans)
    blocks = {}
    for far in range(2, pix, 2):
        blocks[far] = hop(own, far, True)
        odd = hop(own[cut:], far ^ 1, True)
        if cut:
            odd = (hop(blocks[far][:cut], 1, False), odd)
        blocks[far ^ 1] = odd if cut else (odd,)
        blocks[far] = (blocks[far],)
    blocks[1] = (hop(own, 1, True),)
    blocks[0] = (hop(own, 0, True),)
    groups = [[0], [1]] + [[far, far ^ 1][i : i + 1] for far in range(2, pix, 2) for i in range(2)]
    carry = None
    for group in groups:
        carry = fold(own, [(s, blocks[s]) for s in group], carry, group is groups[-1])
    flow, matched = carry
    return flow.reshape(1, 1, 2, rows), matched.reshape(1, 1, rows, chans)


def solution(mesh):
    return jax.shard_map(
        body,
        mesh=mesh,
        in_specs=(P(("clips", "pair"), "dir", "pix", None),),
        out_specs=(
            P(("clips", "pair"), "dir", None, "pix"),
            P(("clips", "pair"), "dir", "pix", None),
        ),
        check_vma=False,
    )
```

time: 27.3 us -> 18.8 us (0.69)
  blocking collectives: 17.3 us -> 0 us
  waiting for transfers between devices: 0.45 us -> 6.62 us
  Pallas kernels: 0 us -> 4.86 us
  starting transfers between devices: 1.19 us -> 5.51 us
  other arithmetic: 2.18 us -> 0 us
  matrix products: 2.06 us -> 0 us
  loops' own time: 1.38 us -> 0 us
  local copies, waits for them, and re-layouts: 1.84 us -> 0.96 us
    all_gather x1 -> x0, blocking collectives: 17.3 us -> none  [body(): lax.all_gather(features, 'pix', axis=2, tiled=True)]
    ppermute x3 -> x4, waiting for transfers between devices: 0.45 us -> 6.62 us  [hop(): return lax.ppermute(array, ('pix', 'dir'), pairs)]
    pallas_call x0 -> x4, Pallas kernels: none -> 4.86 us  [fold(): pl.pallas_call(functools.partial(fold_kernel, shifts, counts, first, last...]
    ppermute x3 -> x4, starting transfers between devices: 1.19 us -> 5.51 us  [hop(): return lax.ppermute(array, ('pix', 'dir'), pairs)]
    dot_general x4 -> x0, matrix products: 2.06 us -> none  [the longest x2 1.07 us: fold_part(): jnp.dot(weights.astype(jnp.bfloat16), keys, preferred_element_type=jnp.fl...]
    another operation x1 -> x0, loops' own time: 1.38 us -> none  [make_step(): lax.scan(inner, carry, (blocks, jnp.arange(length // width, dtype=jnp.int...]
    reduce_sum x2 -> x0, other arithmetic: 1.29 us -> none  [fold_part(): sum_y = sum_y * fade + jnp.sum(weights * posy[None, :], axis=1)]
    dynamic_slice x2 -> x0, local copies, waits for them, and re-layouts: 1.17 us -> none  [make_step(): lax.scan(inner, carry, (blocks, jnp.arange(length // width, dtype=jnp.int...]
  transfers between devices with their start and end apart: 3 -> 4, of which waited for: 1 -> 1; matrix products, arithmetic and copies ran while one was open for 3% -> 0% of each run, Pallas kernels for 0% -> 16%
where the time goes in v1:
time: 18.8 us; the launch traced here: 18.6 us
  waiting for transfers between devices  6.62 us (35%)
  starting transfers between devices  5.51 us (29%)
  Pallas kernels  4.86 us (26%)
  local copies, waits for them, and re-layouts  0.96 us (5%)
  between operations  0.67 us (4%)
    ppermute x4, waiting for transfers between devices, hop(): return lax.ppermute(array, ('pix', 'dir'), pairs)  6.62 us
    ppermute x4, starting transfers between devices, hop(): return lax.ppermute(array, ('pix', 'dir'), pairs)  5.51 us
    pallas_call x4, Pallas kernels, fold(): pl.pallas_call(functools.partial(fold_kernel, shifts, counts, first, last...  4.86 us
    unnamed x2, local copies, waits for them, and re-layouts  0.96 us
  transfers between devices with their start and end apart: 4, of which 1 were waited for; matrix products, arithmetic and copies ran while one was open for 0% of the time, Pallas kernels for 16%

profile of v1, /device:TPU:0, one launch (start us, length us, event | category | flops | bytes accessed | tf_op | source)
XLA Modules:
  0.0 18.6 jit_solution(18416541468795315583)
XLA Ops:
  0.6 0.6 %collective-permute-start.3 = (bf16[480,128]{1,0:T(8,128)(2,1)}, bf16[480,128]{1,0:T(8,128)(2,1)S(1)}, u32[]{:S(2)}, u32[]{:S(2)}) collective-permute-start(bf16[480,128]{1,0:T(8,128)(2,1)} %bitcast.3), channel_id=1, source_target_pairs={{0,1},{1,0},{4,5},{5,4},{8,9},{9,8},{12,13},{13,12},{2,3},{3,2},{6... | collective-permute-start | bytes 368648 | tf_op jit(solution)/shard_map/ppermute | solution.py:22
  1.2 2.7 %collective-permute-start.2 = (bf16[480,128]{1,0:T(8,128)(2,1)}, bf16[480,128]{1,0:T(8,128)(2,1)S(1)}, u32[]{:S(2)}, u32[]{:S(2)}) collective-permute-start(bf16[480,128]{1,0:T(8,128)(2,1)} %bitcast.4), channel_id=1, source_target_pairs={{0,5},{1,4},{4,1},{5,0},{8,13},{9,12},{12,9},{13,8},{2,7},{3,6},{6... | collective-permute-start | bytes 368648 | tf_op jit(solution)/shard_map/ppermute | solution.py:22
  3.9 2.3 %collective-permute-start.1 = (bf16[480,128]{1,0:T(8,128)(2,1)}, bf16[480,128]{1,0:T(8,128)(2,1)S(1)}, u32[]{:S(2)}, u32[]{:S(2)}) collective-permute-start(bf16[480,128]{1,0:T(8,128)(2,1)} %bitcast.5), channel_id=1, source_target_pairs={{0,9},{1,8},{4,13},{5,12},{8,1},{9,0},{12,5},{13,4},{2,11},{3,10},... | collective-permute-start | bytes 368648 | tf_op jit(solution)/shard_map/ppermute | solution.py:22
  6.1 0.0 collective-permute-start
  6.1 0.0 collective-permute-done.3.refs_1_
  6.1 0.0 copy-start
  6.1 1.0 %copy-done = bf16[1,1,480,128]{3,2,1,0:T(8,128)(2,1)S(1)} copy-done((bf16[1,1,480,128]{3,2,1,0:T(8,128)(2,1)S(1)}, bf16[1,1,480,128]{3,2,1,0:T(8,128)(2,1)}, u32[]{:S(2)}) %copy-start) | copy-done | bytes 122904
  7.1 0.7 %shard_map.30 = (f32[480,128]{1,0:T(8,128)S(1)}, f32[480,256]{1,0:T(8,128)S(1)}, bf16[480,128]{1,0:T(8,128)(2,1)S(1)}) custom-call(bf16[480,128]{1,0:T(8,128)(2,1)S(1)} %bitcast.7, bf16[480,128]{1,0:T(8,128)(2,1)S(1)} %collective-permute-done.3.refs_1_), custom_call_target="tpu_custom_call" | custom-call | flops 176947200 | bytes 122880 | tf_op jit(solution)/shard_map/pallas_call | solution.py:96
  7.8 0.0 collective-permute-done.2.refs_1_
  7.9 1.1 %shard_map.31 = (f32[480,128]{1,0:T(8,128)S(1)}, f32[480,256]{1,0:T(8,128)S(1)}) custom-call(bf16[480,128]{1,0:T(8,128)(2,1)S(1)} %bitcast.8, bf16[480,128]{1,0:T(8,128)(2,1)S(1)} %collective-permute-done.2.refs_1_, f32[480,128]{1,0:T(8,128)S(1)} %get-tuple-element.11.refs_2_, f32[480,256]{1,0:T(8,128)S(1)} %get-tuple-element.12.refs_3_, ...), custom_call_target="tpu_custom_call" | custom-call | flops 176947200 | bytes 122880 | tf_op jit(solution)/shard_map/pallas_call | solution.py:96
  9.0 6.6 %collective-permute-done.1.refs_1_ = bf16[480,128]{1,0:T(8,128)(2,1)S(1)} collective-permute-done((bf16[480,128]{1,0:T(8,128)(2,1)}, bf16[480,128]{1,0:T(8,128)(2,1)S(1)}, u32[]{:S(2)}, u32[]{:S(2)}) %collective-permute-start.1) | collective-permute-done | bytes 122912 | tf_op jit(solution)/shard_map/ppermute | solution.py:22
  15.6 1.1 %shard_map.32 = (f32[480,128]{1,0:T(8,128)S(1)}, f32[480,256]{1,0:T(8,128)S(1)}) custom-call(bf16[480,128]{1,0:T(8,128)(2,1)S(1)} %bitcast.9, bf16[480,128]{1,0:T(8,128)(2,1)S(1)} %collective-permute-done.1.refs_1_, f32[480,128]{1,0:T(8,128)S(1)} %get-tuple-element.14.refs_2_, f32[480,256]{1,0:T(8,128)S(1)} %get-tuple-element.15.refs_3_, ...), custom_call_target="tpu_custom_call" | custom-call | flops 176947200 | bytes 122880 | tf_op jit(solution)/shard_map/pallas_call | solution.py:96
  16.7 0.0 collective-permute-done.refs_1_
  16.7 1.9 %shard_map.33 = (f32[2,480]{1,0:T(2,128)}, bf16[480,128]{1,0:T(8,128)(2,1)}) custom-call(bf16[480,128]{1,0:T(8,128)(2,1)S(1)} %bitcast.10, bf16[480,128]{1,0:T(8,128)(2,1)S(1)} %collective-permute-done.refs_1_, f32[480,128]{1,0:T(8,128)S(1)} %get-tuple-element.16.refs_2_, f32[480,256]{1,0:T(8,128)S(1)} %get-tuple-element.17.refs_3_, ...), custom_call_target="tpu_custom_call" | custom-call | flops 176947200 | bytes 122880 | tf_op jit(solution)/shard_map/pallas_call | solution.py:96
Async XLA Ops:
  0.6 5.5 %collective-permute-start.3 = (bf16[480,128]{1,0:T(8,128)(2,1)}, bf16[480,128]{1,0:T(8,128)(2,1)S(1)}, u32[]{:S(2)}, u32[]{:S(2)}) collective-permute-start(bf16[480,128]{1,0:T(8,128)(2,1)} %bitcast.3), channel_id=1, source_target_pairs={{0,1},{1,0},{4,5},{5,4},{8,9},{9,8},{12,13},{13,12},{2,3},{3,2},{6... | collective-permute-start | bytes 368648 | tf_op jit(solution)/shard_map/ppermute | solution.py:22
  1.2 6.7 %collective-permute-start.2 = (bf16[480,128]{1,0:T(8,128)(2,1)}, bf16[480,128]{1,0:T(8,128)(2,1)S(1)}, u32[]{:S(2)}, u32[]{:S(2)}) collective-permute-start(bf16[480,128]{1,0:T(8,128)(2,1)} %bitcast.4), channel_id=1, source_target_pairs={{0,5},{1,4},{4,1},{5,0},{8,13},{9,12},{12,9},{13,8},{2,7},{3,6},{6... | collective-permute-start | bytes 368648 | tf_op jit(solution)/shard_map/ppermute | solution.py:22
  3.9 11.7 %collective-permute-start.1 = (bf16[480,128]{1,0:T(8,128)(2,1)}, bf16[480,128]{1,0:T(8,128)(2,1)S(1)}, u32[]{:S(2)}, u32[]{:S(2)}) collective-permute-start(bf16[480,128]{1,0:T(8,128)(2,1)} %bitcast.5), channel_id=1, source_target_pairs={{0,9},{1,8},{4,13},{5,12},{8,1},{9,0},{12,5},{13,4},{2,11},{3,10},... | collective-permute-start | bytes 368648 | tf_op jit(solution)/shard_map/ppermute | solution.py:22
  6.1 10.6 %collective-permute-start = (bf16[480,128]{1,0:T(8,128)(2,1)}, bf16[480,128]{1,0:T(8,128)(2,1)S(1)}, u32[]{:S(2)}, u32[]{:S(2)}) collective-permute-start(bf16[480,128]{1,0:T(8,128)(2,1)} %bitcast.6), channel_id=1, source_target_pairs={{0,13},{1,12},{4,9},{5,8},{8,5},{9,4},{12,1},{13,0},{2,15},{3,14},... | collective-permute-start | bytes 368648 | tf_op jit(solution)/shard_map/ppermute | solution.py:22
  6.1 1.0 %copy-start = (bf16[1,1,480,128]{3,2,1,0:T(8,128)(2,1)S(1)}, bf16[1,1,480,128]{3,2,1,0:T(8,128)(2,1)}, u32[]{:S(2)}) copy-start(bf16[1,1,480,128]{3,2,1,0:T(8,128)(2,1)} %param.1) | copy-start | bytes 368644

commit v2 on v1

v2 whole, which is shorter than its diff:
```python
import functools
import math

import jax
import jax.numpy as jnp
from jax import lax
from jax.experimental import pallas as pl
from jax.experimental.pallas import tpu as pltpu
from jax.sharding import PartitionSpec as P

W = 120
VMEM = pl.BlockSpec(memory_space=pltpu.VMEM)
ANY = pl.BlockSpec(memory_space=pl.ANY)
PARAMS = pltpu.CompilerParams(vmem_limit_bytes=24 * 1024 * 1024)


def hop(array, targets, cross):
    frames = lax.axis_size("dir")
    flip = 1 if cross else 0
    pairs = [
        (z * frames + d, t * frames + (d ^ flip))
        for z, t in enumerate(targets)
        if t is not None
        for d in range(frames)
    ]
    return lax.ppermute(array, ("pix", "dir"), pairs)


def pick(table):
    here = lax.axis_index("pix")
    value = jnp.int32(0)
    for z, entry in enumerate(table):
        value = jnp.where(here == z, entry, value)
    return value


def places_kernel(out_ref):
    rows, chans = out_ref.shape
    column = lax.broadcasted_iota(jnp.int32, (rows, chans), 1)
    index = lax.broadcasted_iota(jnp.int32, (rows, chans), 0).astype(jnp.float32)
    row = jnp.floor((index + 0.5) * (1.0 / W))
    place = index - row * W
    values = jnp.where(column == 0, place, jnp.where(column == 1, row, 1.0))
    out_ref[...] = jnp.where(column < 3, values, 0.0).astype(jnp.bfloat16)


def places(rows, chans):
    return pl.pallas_call(
        places_kernel,
        out_shape=jax.ShapeDtypeStruct((rows, chans), jnp.bfloat16),
        out_specs=VMEM,
        compiler_params=PARAMS,
        cost_estimate=pl.CostEstimate(flops=rows * chans, bytes_accessed=0, transcendentals=0),
    )()


def fold_kernel(blocks, spans, first, last, *refs):
    refs = list(refs)
    q_ref = refs.pop(0)
    key_refs = [[refs.pop(0) for _ in range(n)] for _, n in blocks]
    places_ref = refs.pop(0)
    if not first:
        top_in, acc_in = refs.pop(0), refs.pop(0)
    rows, chans = q_ref.shape
    scale = chans ** (-0.5) * math.log2(math.e)
    here = lax.axis_index("pix")
    column = lax.broadcasted_iota(jnp.int32, (1, chans), 1)
    keys, values = [], []
    for (table, _), held in zip(blocks, key_refs):
        part = held[0][...]
        if len(held) > 1:
            part = jnp.where((here == 0) | (here == len(table) - 1), held[1][...], part)
        start_row = pick(table) * (part.shape[0] // W)
        offset = jnp.where(column == 1, start_row, 0).astype(jnp.float32).astype(jnp.bfloat16)
        keys.append(part)
        values.append(jnp.concatenate([part, places_ref[...] + offset], axis=1))
    keys = jnp.concatenate(keys, axis=0) if len(keys) > 1 else keys[0]
    values = jnp.concatenate(values, axis=0) if len(values) > 1 else values[0]
    count = keys.shape[0]
    scores = [
        lax.dot_general(
            q_ref[begin:end, :], keys, (((1,), (1,)), ((), ())), preferred_element_type=jnp.float32
        )
        for begin, end in spans
    ]
    tops, fades, weights = [], [], []
    for score, (begin, end) in zip(scores, spans):
        top = jnp.broadcast_to(jnp.max(score, axis=1, keepdims=True), (end - begin, chans))
        if not first:
            old = top_in[begin:end, :]
            top = jnp.maximum(old, top)
            fades.append(jnp.exp2((old - top) * scale))
        tops.append(top)
        parts = [
            jnp.exp2((score[:, j : j + chans] - top[:, : min(chans, count - j)]) * scale).astype(jnp.bfloat16)
            for j in range(0, count, chans)
        ]
        weights.append(jnp.concatenate(parts, axis=1) if len(parts) > 1 else parts[0])
    accs = [jnp.dot(weight, values, preferred_element_type=jnp.float32) for weight in weights]
    if not first:
        accs = [
            acc + acc_in[begin:end, :] * jnp.concatenate([fade, fade], axis=1)
            for acc, fade, (begin, end) in zip(accs, fades, spans)
        ]
    if not last:
        top_out, acc_out = refs
        for acc, top, (begin, end) in zip(accs, tops, spans):
            top_out[begin:end, :] = top
            acc_out[begin:end, :] = acc
        return
    flow_hbm, matched_hbm, flow_ref, matched_ref, sems = refs
    copies = []
    for place, (acc, (begin, end)) in enumerate(zip(accs, spans)):
        inverse = 1.0 / acc[:, chans + 2 : chans + 3]
        matched_ref[begin:end, :] = (acc[:, :chans] * inverse).astype(jnp.bfloat16)
        copies.append(
            pltpu.make_async_copy(
                matched_ref.at[begin:end, :], matched_hbm.at[begin:end, :], sems.at[place]
            )
        )
        copies[-1].start()
        sums = jnp.transpose(acc[:, chans:] * inverse)[:2, :]
        index = here * rows + begin + lax.broadcasted_iota(jnp.int32, (1, end - begin), 1)
        index = index.astype(jnp.float32)
        own_row = jnp.floor((index + 0.5) * (1.0 / W))
        own = jnp.concatenate([index - own_row * W, own_row], axis=0)
        flow_ref[:, begin:end] = (sums - own) * (1.0 / W)
    copies.append(pltpu.make_async_copy(flow_ref, flow_hbm, sems.at[len(spans)]))
    copies[-1].start()
    for copy in copies:
        copy.wait()


def fold(queries, positions, blocks, carry, last):
    rows, chans = queries.shape
    first = carry is None
    middle = (rows // 2 + 127) // 128 * 128
    spans = [(0, middle), (middle, rows)] if middle < rows else [(0, rows)]
    operands = [queries, *[part for _, held in blocks for part in held], positions, *(carry or ())]
    keys = sum(held[0].shape[0] for _, held in blocks)
    if last:
        shapes = ((2, rows), jnp.float32), ((rows, chans), jnp.bfloat16)
        scratch = [pltpu.VMEM(shape, kind) for shape, kind in shapes]
        scratch.append(pltpu.SemaphoreType.DMA((len(spans) + 1,)))
    else:
        shapes = ((rows, chans), jnp.float32), ((rows, 2 * chans), jnp.float32)
        scratch = []
    return pl.pallas_call(
        functools.partial(fold_kernel, [(table, len(held)) for table, held in blocks], spans, first, last),
        out_shape=[jax.ShapeDtypeStruct(shape, kind) for shape, kind in shapes],
        in_specs=[VMEM] * len(operands),
        out_specs=[ANY if last else VMEM] * len(shapes),
        scratch_shapes=scratch,
        compiler_params=PARAMS,
        cost_estimate=pl.CostEstimate(
            flops=6 * rows * keys * chans, bytes_accessed=2 * keys * chans, transcendentals=rows * keys
        ),
    )(*operands)


def sources_of(targets):
    return [targets.index(z) for z in range(len(targets))]


def body(features):
    rows, chans = features.shape[2:]
    pix = lax.axis_size("pix")
    straight = list(range(pix))
    own = features.reshape(rows, chans)

    def send(array, targets, cross=True):
        return hop(array, targets, cross)

    positions = places(rows, chans)
    if pix == 4:
        far = send(own, [2, 0, 3, 1])
        back = send(own, [1, 3, 0, 2])
        zero = send(own, straight)
        mid = send(own, [0, 2, 1, 3])
        relay = send(far, [1, 0, 3, 2], False)
        groups = [
            [(straight, [zero])],
            [(sources_of([2, 0, 3, 1]), [far])],
            [(sources_of([1, 3, 0, 2]), [back])],
            [(straight[::-1], [mid, relay])],
        ]
    else:
        groups = []
        for shift in range(pix):
            targets = [(z + shift) % pix for z in range(pix)]
            groups.append([(sources_of(targets), [send(own, targets)])])
    carry = None
    for place, blocks in enumerate(groups):
        carry = fold(own, positions, blocks, carry, place == len(groups) - 1)
    flow, matched = carry
    return flow.reshape(1, 1, 2, rows), matched.reshape(1, 1, rows, chans)


def solution(mesh):
    return jax.shard_map(
        body,
        mesh=mesh,
        in_specs=(P(("clips", "pair"), "dir", "pix", None),),
        out_specs=(
            P(("clips", "pair"), "dir", None, "pix"),
            P(("clips", "pair"), "dir", "pix", None),
        ),
        check_vma=False,
    )
```

time: 18.8 us -> 16.8 us (0.89)
  Pallas kernels: 4.86 us -> 3.38 us
  local copies, waits for them, and re-layouts: 0.96 us -> 0.01 us
  starting transfers between devices: 5.51 us -> 6.26 us
  waiting for transfers between devices: 6.62 us -> 6.31 us
    pallas_call x4 -> x5, Pallas kernels: 4.86 us -> 3.38 us  [the longest x4 3.29 us: fold(): pl.pallas_call(functools.partial(fold_kernel, [(table, len(held)) for tab...]
    unnamed x2, local copies, waits for them, and re-layouts: 0.96 us -> 0.01 us
    ppermute x4 -> x5, starting transfers between devices: 5.51 us -> 6.26 us  [hop(): return lax.ppermute(array, ('pix', 'dir'), pairs)]
    ppermute x4 -> x5, waiting for transfers between devices: 6.62 us -> 6.31 us  [hop(): return lax.ppermute(array, ('pix', 'dir'), pairs)]
  transfers between devices with their start and end apart: 4 -> 5, of which waited for: 1 -> 3; matrix products, arithmetic and copies ran while one was open for 0% -> 0% of each run, Pallas kernels for 16% -> 12%
where the time goes in v2:
time: 16.8 us; the launch traced here: 16.6 us
  waiting for transfers between devices  6.31 us (38%)
  starting transfers between devices  6.26 us (37%)
  Pallas kernels  3.38 us (20%)
  between operations  0.69 us (4%)
    ppermute x5, waiting for transfers between devices, hop(): return lax.ppermute(array, ('pix', 'dir'), pairs)  6.31 us
    ppermute x5, starting transfers between devices, hop(): return lax.ppermute(array, ('pix', 'dir'), pairs)  6.26 us
    pallas_call x4, Pallas kernels, fold(): pl.pallas_call(functools.partial(fold_kernel, [(table, len(held)) for tab...  3.29 us
  transfers between devices with their start and end apart: 5, of which 3 were waited for; matrix products, arithmetic and copies ran while one was open for 0% of the time, Pallas kernels for 12%

profile of v2, /device:TPU:0, one launch (start us, length us, event | category | flops | bytes accessed | tf_op | source)
XLA Modules:
  0.0 16.6 jit_solution(14952220704910283125)
XLA Ops:
  0.6 0.0 copy-start
  0.6 3.6 %collective-permute-start.1 = (bf16[480,128]{1,0:T(8,128)(2,1)}, bf16[480,128]{1,0:T(8,128)(2,1)S(1)}, u32[]{:S(2)}, u32[]{:S(2)}) collective-permute-start(bf16[480,128]{1,0:T(8,128)(2,1)} %bitcast.3), channel_id=1, source_target_pairs={{0,9},{1,8},{4,1},{5,0},{8,13},{9,12},{12,5},{13,4},{2,11},{3,10},... | collective-permute-start | bytes 368648 | tf_op jit(solution)/shard_map/ppermute | solution.py:26
  4.2 0.7 %collective-permute-start.4 = (bf16[480,128]{1,0:T(8,128)(2,1)}, bf16[480,128]{1,0:T(8,128)(2,1)S(1)}, u32[]{:S(2)}, u32[]{:S(2)}) collective-permute-start(bf16[480,128]{1,0:T(8,128)(2,1)} %bitcast.4), channel_id=1, source_target_pairs={{0,1},{1,0},{4,5},{5,4},{8,9},{9,8},{12,13},{13,12},{2,3},{3,2},{6... | collective-permute-start | bytes 368648 | tf_op jit(solution)/shard_map/ppermute | solution.py:26
  4.9 0.0 collective-permute-start.3
  4.9 0.0 collective-permute-start
  4.9 3.4 %collective-permute-done.1.refs_1_ = bf16[480,128]{1,0:T(8,128)(2,1)S(1)} collective-permute-done((bf16[480,128]{1,0:T(8,128)(2,1)}, bf16[480,128]{1,0:T(8,128)(2,1)S(1)}, u32[]{:S(2)}, u32[]{:S(2)}) %collective-permute-start.1) | collective-permute-done | bytes 122912 | tf_op jit(solution)/shard_map/ppermute | solution.py:26
  8.3 2.0 %collective-permute-start.2 = (bf16[480,128]{1,0:T(8,128)(2,1)S(1)}, bf16[480,128]{1,0:T(8,128)(2,1)S(1)}, u32[]{:S(2)}, u32[]{:S(2)}) collective-permute-start(bf16[480,128]{1,0:T(8,128)(2,1)S(1)} %collective-permute-done.1.refs_1_), channel_id=1, source_target_pairs={{0,4},{1,5},{4,0},{5,1},{8,12},{9,13},{12,8},{13,9},{2,6},{3,7},{6... | collective-permute-start | bytes 368648 | tf_op jit(solution)/shard_map/ppermute | solution.py:26
  10.3 0.1 shard_map.30.refs_2_.refs_3_
  10.4 0.0 collective-permute-done.4.refs_1_
  10.4 0.0 copy-done
  10.4 0.6 %shard_map.31 = (f32[480,128]{1,0:T(8,128)S(1)}, f32[480,256]{1,0:T(8,128)S(1)}) custom-call(bf16[480,128]{1,0:T(8,128)(2,1)S(1)} %bitcast.7, bf16[480,128]{1,0:T(8,128)(2,1)S(1)} %collective-permute-done.4.refs_1_, bf16[480,128]{1,0:T(8,128)(2,1)S(1)} %shard_map.30.refs_2_.refs_3_), custom_call_target="tpu_custom_call" | custom-call | flops 176947200 | bytes 122880 | tf_op jit(solution)/shard_map/pallas_call | solution.py:148
  11.0 0.6 %shard_map.32 = (f32[480,128]{1,0:T(8,128)S(1)}, f32[480,256]{1,0:T(8,128)S(1)}) custom-call(bf16[480,128]{1,0:T(8,128)(2,1)S(1)} %bitcast.8, bf16[480,128]{1,0:T(8,128)(2,1)S(1)} %collective-permute-done.1.refs_1_, bf16[480,128]{1,0:T(8,128)(2,1)S(1)} %shard_map.30.refs_2_.refs_3_, f32[480,128]{1,0:T(8,128)S(1)} %get-tuple-element.10.refs_3_, ...), custom_call_target="tpu_custom_call" | custom-call | flops 176947200 | bytes 122880 | tf_op jit(solution)/shard_map/pallas_call | solution.py:148
  11.6 1.0 %collective-permute-done.3.refs_1_ = bf16[480,128]{1,0:T(8,128)(2,1)S(1)} collective-permute-done((bf16[480,128]{1,0:T(8,128)(2,1)}, bf16[480,128]{1,0:T(8,128)(2,1)S(1)}, u32[]{:S(2)}, u32[]{:S(2)}) %collective-permute-start.3) | collective-permute-done | bytes 122912 | tf_op jit(solution)/shard_map/ppermute | solution.py:26
  12.6 0.6 %shard_map.33 = (f32[480,128]{1,0:T(8,128)S(1)}, f32[480,256]{1,0:T(8,128)S(1)}) custom-call(bf16[480,128]{1,0:T(8,128)(2,1)S(1)} %bitcast.9, bf16[480,128]{1,0:T(8,128)(2,1)S(1)} %collective-permute-done.3.refs_1_, bf16[480,128]{1,0:T(8,128)(2,1)S(1)} %shard_map.30.refs_2_.refs_3_, f32[480,128]{1,0:T(8,128)S(1)} %get-tuple-element.12.refs_3_, ...), custom_call_target="tpu_custom_call" | custom-call | flops 176947200 | bytes 122880 | tf_op jit(solution)/shard_map/pallas_call | solution.py:148
  13.2 0.0 collective-permute-done.refs_1_
  13.2 1.9 %collective-permute-done.2.refs_2_ = bf16[480,128]{1,0:T(8,128)(2,1)S(1)} collective-permute-done((bf16[480,128]{1,0:T(8,128)(2,1)S(1)}, bf16[480,128]{1,0:T(8,128)(2,1)S(1)}, u32[]{:S(2)}, u32[]{:S(2)}) %collective-permute-start.2) | collective-permute-done | bytes 122912 | tf_op jit(solution)/shard_map/ppermute | solution.py:26
  15.2 1.5 %shard_map.34 = (f32[2,480]{1,0:T(2,128)}, bf16[480,128]{1,0:T(8,128)(2,1)}) custom-call(bf16[480,128]{1,0:T(8,128)(2,1)S(1)} %bitcast.10, bf16[480,128]{1,0:T(8,128)(2,1)S(1)} %collective-permute-done.refs_1_, bf16[480,128]{1,0:T(8,128)(2,1)S(1)} %collective-permute-done.2.refs_2_, bf16[480,128]{1,0:T(8,128)(2,1)S(1)} %shard_map.30.refs_2_.refs_3_, ...), custom_call_target="tpu_custom_call" | custom-call | flops 176947200 | bytes 122880 | tf_op jit(solution)/shard_map/pallas_call | solution.py:148
Async XLA Ops:
  0.6 9.8 %copy-start = (bf16[1,1,480,128]{3,2,1,0:T(8,128)(2,1)S(1)}, bf16[1,1,480,128]{3,2,1,0:T(8,128)(2,1)}, u32[]{:S(2)}) copy-start(bf16[1,1,480,128]{3,2,1,0:T(8,128)(2,1)} %param.1) | copy-start | bytes 368644
  0.6 7.6 %collective-permute-start.1 = (bf16[480,128]{1,0:T(8,128)(2,1)}, bf16[480,128]{1,0:T(8,128)(2,1)S(1)}, u32[]{:S(2)}, u32[]{:S(2)}) collective-permute-start(bf16[480,128]{1,0:T(8,128)(2,1)} %bitcast.3), channel_id=1, source_target_pairs={{0,9},{1,8},{4,1},{5,0},{8,13},{9,12},{12,5},{13,4},{2,11},{3,10},... | collective-permute-start | bytes 368648 | tf_op jit(solution)/shard_map/ppermute | solution.py:26
  4.2 6.2 %collective-permute-start.4 = (bf16[480,128]{1,0:T(8,128)(2,1)}, bf16[480,128]{1,0:T(8,128)(2,1)S(1)}, u32[]{:S(2)}, u32[]{:S(2)}) collective-permute-start(bf16[480,128]{1,0:T(8,128)(2,1)} %bitcast.4), channel_id=1, source_target_pairs={{0,1},{1,0},{4,5},{5,4},{8,9},{9,8},{12,13},{13,12},{2,3},{3,2},{6... | collective-permute-start | bytes 368648 | tf_op jit(solution)/shard_map/ppermute | solution.py:26
  4.9 7.8 %collective-permute-start.3 = (bf16[480,128]{1,0:T(8,128)(2,1)}, bf16[480,128]{1,0:T(8,128)(2,1)S(1)}, u32[]{:S(2)}, u32[]{:S(2)}) collective-permute-start(bf16[480,128]{1,0:T(8,128)(2,1)} %bitcast.5), channel_id=1, source_target_pairs={{0,5},{1,4},{4,13},{5,12},{8,1},{9,0},{12,9},{13,8},{2,7},{3,6},{6... | collective-permute-start | bytes 368648 | tf_op jit(solution)/shard_map/ppermute | solution.py:26
  4.9 8.4 %collective-permute-start = (bf16[480,128]{1,0:T(8,128)(2,1)}, bf16[480,128]{1,0:T(8,128)(2,1)S(1)}, u32[]{:S(2)}, u32[]{:S(2)}) collective-permute-start(bf16[480,128]{1,0:T(8,128)(2,1)} %bitcast.6), channel_id=1, source_target_pairs={{0,1},{1,0},{4,9},{5,8},{8,5},{9,4},{12,13},{13,12},{2,3},{3,2},{6... | collective-permute-start | bytes 368648 | tf_op jit(solution)/shard_map/ppermute | solution.py:26
  8.3 6.9 %collective-permute-start.2 = (bf16[480,128]{1,0:T(8,128)(2,1)S(1)}, bf16[480,128]{1,0:T(8,128)(2,1)S(1)}, u32[]{:S(2)}, u32[]{:S(2)}) collective-permute-start(bf16[480,128]{1,0:T(8,128)(2,1)S(1)} %collective-permute-done.1.refs_1_), channel_id=1, source_target_pairs={{0,4},{1,5},{4,0},{5,1},{8,12},{9,13},{12,8},{13,9},{2,6},{3,7},{6... | collective-permute-start | bytes 368648 | tf_op jit(solution)/shard_map/ppermute | solution.py:26

commit v3 on v2

--- a/solution.py
+++ b/solution.py
@@ -34,30 +34,37 @@
     return value
 
 
-def places_kernel(out_ref):
-    rows, chans = out_ref.shape
+def prepare_kernel(own_ref, whole_ref, places_ref, *part_refs):
+    whole_ref[...] = own_ref[...]
+    begin = 0
+    for ref in part_refs:
+        ref[...] = own_ref[begin : begin + ref.shape[0], :]
+        begin += ref.shape[0]
+    rows, chans = places_ref.shape
     column = lax.broadcasted_iota(jnp.int32, (rows, chans), 1)
     index = lax.broadcasted_iota(jnp.int32, (rows, chans), 0).astype(jnp.float32)
     row = jnp.floor((index + 0.5) * (1.0 / W))
     place = index - row * W
     values = jnp.where(column == 0, place, jnp.where(column == 1, row, 1.0))
-    out_ref[...] = jnp.where(column < 3, values, 0.0).astype(jnp.bfloat16)
-
-
-def places(rows, chans):
+    places_ref[...] = jnp.where(column < 3, values, 0.0).astype(jnp.bfloat16)
+
+
+def prepare(own, sizes):
+    rows, chans = own.shape
     return pl.pallas_call(
-        places_kernel,
-        out_shape=jax.ShapeDtypeStruct((rows, chans), jnp.bfloat16),
-        out_specs=VMEM,
+        prepare_kernel,
+        out_shape=[jax.ShapeDtypeStruct((size, chans), own.dtype) for size in (rows, rows, *sizes)],
+        in_specs=[VMEM],
+        out_specs=[VMEM] * (2 + len(sizes)),
         compiler_params=PARAMS,
-        cost_estimate=pl.CostEstimate(flops=rows * chans, bytes_accessed=0, transcendentals=0),
-    )()
+        cost_estimate=pl.CostEstimate(flops=rows * chans, bytes_accessed=4 * own.size, transcendentals=0),
+    )(own)
 
 
 def fold_kernel(blocks, spans, first, last, *refs):
     refs = list(refs)
     q_ref = refs.pop(0)
-    key_refs = [[refs.pop(0) for _ in range(n)] for _, n in blocks]
+    key_refs = [[refs.pop(0) for _ in range(n)] for _, _, n in blocks]
     places_ref = refs.pop(0)
     if not first:
         top_in, acc_in = refs.pop(0), refs.pop(0)
@@ -66,14 +73,15 @@
     here = lax.axis_index("pix")
     column = lax.broadcasted_iota(jnp.int32, (1, chans), 1)
     keys, values = [], []
-    for (table, _), held in zip(blocks, key_refs):
+    for (table, begin, _), held in zip(blocks, key_refs):
         part = held[0][...]
         if len(held) > 1:
             part = jnp.where((here == 0) | (here == len(table) - 1), held[1][...], part)
-        start_row = pick(table) * (part.shape[0] // W)
+        start_row = pick(table) * (rows // W)
         offset = jnp.where(column == 1, start_row, 0).astype(jnp.float32).astype(jnp.bfloat16)
         keys.append(part)
-        values.append(jnp.concatenate([part, places_ref[...] + offset], axis=1))
+        place = places_ref[begin : begin + part.shape[0], :]
+        values.append(jnp.concatenate([part, place + offset], axis=1))
     keys = jnp.concatenate(keys, axis=0) if len(keys) > 1 else keys[0]
     values = jnp.concatenate(values, axis=0) if len(values) > 1 else values[0]
     count = keys.shape[0]
@@ -136,8 +144,8 @@
     first = carry is None
     middle = (rows // 2 + 127) // 128 * 128
     spans = [(0, middle), (middle, rows)] if middle < rows else [(0, rows)]
-    operands = [queries, *[part for _, held in blocks for part in held], positions, *(carry or ())]
-    keys = sum(held[0].shape[0] for _, held in blocks)
+    operands = [queries, *[part for _, _, held in blocks for part in held], positions, *(carry or ())]
+    keys = sum(held[0].shape[0] for _, _, held in blocks)
     if last:
         shapes = ((2, rows), jnp.float32), ((rows, chans), jnp.bfloat16)
         scratch = [pltpu.VMEM(shape, kind) for shape, kind in shapes]
@@ -146,7 +154,7 @@
         shapes = ((rows, chans), jnp.float32), ((rows, 2 * chans), jnp.float32)
         scratch = []
     return pl.pallas_call(
-        functools.partial(fold_kernel, [(table, len(held)) for table, held in blocks], spans, first, last),
+        functools.partial(fold_kernel, [(table, begin, len(held)) for table, begin, held in blocks], spans, first, last),
         out_shape=[jax.ShapeDtypeStruct(shape, kind) for shape, kind in shapes],
         in_specs=[VMEM] * len(operands),
         out_specs=[ANY if last else VMEM] * len(shapes),
@@ -171,27 +179,30 @@
     def send(array, targets, cross=True):
         return hop(array, targets, cross)
 
-    positions = places(rows, chans)
+    cut = rows * 8 // 240 * 16
+    queries, positions, head, tail = prepare(own, (cut, rows - cut))
     if pix == 4:
         far = send(own, [2, 0, 3, 1])
         back = send(own, [1, 3, 0, 2])
+        cross = send(tail, [3, 2, 1, 0])
         zero = send(own, straight)
-        mid = send(own, [0, 2, 1, 3])
-        relay = send(far, [1, 0, 3, 2], False)
+        mid = send(head, [0, 2, 1, 3])
+        relay = send(far[:cut], [1, 0, 3, 2], False)
         groups = [
-            [(straight, [zero])],
-            [(sources_of([2, 0, 3, 1]), [far])],
-            [(sources_of([1, 3, 0, 2]), [back])],
-            [(straight[::-1], [mid, relay])],
+            [(straight, 0, [zero])],
+            [(sources_of([2, 0, 3, 1]), 0, [far])],
+            [(sources_of([1, 3, 0, 2]), 0, [back])],
+            [(straight[::-1], cut, [cross])],
+            [(straight[::-1], 0, [mid, relay])],
         ]
     else:
         groups = []
         for shift in range(pix):
             targets = [(z + shift) % pix for z in range(pix)]
-            groups.append([(sources_of(targets), [send(own, targets)])])
+            groups.append([(sources_of(targets), 0, [send(own, targets)])])
     carry = None
     for place, blocks in enumerate(groups):
-        carry = fold(own, positions, blocks, carry, place == len(groups) - 1)
+        carry = fold(queries, positions, blocks, carry, place == len(groups) - 1)
     flow, matched = carry
     return flow.reshape(1, 1, 2, rows), matched.reshape(1, 1, rows, chans)
 

time: 16.8 us -> 18.2 us (1.083)
  starting transfers between devices: 6.26 us -> 8.48 us
  waiting for transfers between devices: 6.31 us -> 4.28 us
  local copies, waits for them, and re-layouts: 0.01 us -> 0.94 us
  Pallas kernels: 3.38 us -> 3.69 us
    ppermute x5 -> x6, starting transfers between devices: 6.26 us -> 8.48 us  [hop(): return lax.ppermute(array, ('pix', 'dir'), pairs)]
    ppermute x5 -> x6, waiting for transfers between devices: 6.31 us -> 4.28 us  [hop(): return lax.ppermute(array, ('pix', 'dir'), pairs)]
    unnamed x2, local copies, waits for them, and re-layouts: 0.01 us -> 0.93 us
    pallas_call x5 -> x6, Pallas kernels: 3.38 us -> 3.69 us  [the longest x5 3.57 us: fold(): pl.pallas_call(functools.partial(fold_kernel, [(table, begin, len(held))...]
  transfers between devices with their start and end apart: 5 -> 6, of which waited for: 3 -> 2; matrix products, arithmetic and copies ran while one was open for 0% -> 0% of each run, Pallas kernels for 12% -> 13%
where the time goes in v3:
time: 18.2 us; the launch traced here: 18.1 us
  starting transfers between devices  8.48 us (47%)
  waiting for transfers between devices  4.28 us (24%)
  Pallas kernels  3.69 us (20%)
  local copies, waits for them, and re-layouts  0.94 us (5%)
  between operations  0.69 us (4%)
    ppermute x6, starting transfers between devices, hop(): return lax.ppermute(array, ('pix', 'dir'), pairs)  8.48 us
    ppermute x6, waiting for transfers between devices, hop(): return lax.ppermute(array, ('pix', 'dir'), pairs)  4.28 us
    pallas_call x5, Pallas kernels, fold(): pl.pallas_call(functools.partial(fold_kernel, [(table, begin, len(held))...  3.57 us
    unnamed x2, local copies, waits for them, and re-layouts  0.93 us
  transfers between devices with their start and end apart: 6, of which 2 were waited for; matrix products, arithmetic and copies ran while one was open for 0% of the time, Pallas kernels for 13%

profile of v3, /device:TPU:0, one launch (start us, length us, event | category | flops | bytes accessed | tf_op | source)
XLA Modules:
  0.0 18.1 jit_solution(2977721709454464630)
XLA Ops:
  0.6 3.6 %collective-permute-start.1 = (bf16[480,128]{1,0:T(8,128)(2,1)}, bf16[480,128]{1,0:T(8,128)(2,1)S(1)}, u32[]{:S(2)}, u32[]{:S(2)}) collective-permute-start(bf16[480,128]{1,0:T(8,128)(2,1)} %bitcast.3), channel_id=1, source_target_pairs={{0,9},{1,8},{4,1},{5,0},{8,13},{9,12},{12,5},{13,4},{2,11},{3,10},... | collective-permute-start | bytes 368648 | tf_op jit(solution)/shard_map/ppermute | solution.py:26
  4.2 0.7 %collective-permute-start.5 = (bf16[480,128]{1,0:T(8,128)(2,1)}, bf16[480,128]{1,0:T(8,128)(2,1)S(1)}, u32[]{:S(2)}, u32[]{:S(2)}) collective-permute-start(bf16[480,128]{1,0:T(8,128)(2,1)} %bitcast.4), channel_id=1, source_target_pairs={{0,1},{1,0},{4,5},{5,4},{8,9},{9,8},{12,13},{13,12},{2,3},{3,2},{6... | collective-permute-start | bytes 368648 | tf_op jit(solution)/shard_map/ppermute | solution.py:26
  4.9 0.0 collective-permute-start.4
  4.9 0.0 copy-start
  4.9 0.9 %copy-done = bf16[1,1,480,128]{3,2,1,0:T(8,128)(2,1)S(1)} copy-done((bf16[1,1,480,128]{3,2,1,0:T(8,128)(2,1)S(1)}, bf16[1,1,480,128]{3,2,1,0:T(8,128)(2,1)}, u32[]{:S(2)}) %copy-start) | copy-done | bytes 122904
  5.8 0.1 shard_map.30
  5.9 0.1 collective-permute-start
  6.0 2.2 %collective-permute-done.1.refs_1_ = bf16[480,128]{1,0:T(8,128)(2,1)S(1)} collective-permute-done((bf16[480,128]{1,0:T(8,128)(2,1)}, bf16[480,128]{1,0:T(8,128)(2,1)S(1)}, u32[]{:S(2)}, u32[]{:S(2)}) %collective-permute-start.1) | collective-permute-done | bytes 122912 | tf_op jit(solution)/shard_map/ppermute | solution.py:26
  8.3 2.0 %collective-permute-start.2 = (bf16[256,128]{1,0:T(8,128)(2,1)S(1)}, bf16[256,128]{1,0:T(8,128)(2,1)S(1)}, u32[]{:S(2)}, u32[]{:S(2)}) collective-permute-start(bf16[256,128]{1,0:T(8,128)(2,1)S(1)} %slice.4), channel_id=1, source_target_pairs={{0,4},{1,5},{4,0},{5,1},{8,12},{9,13},{12,8},{13,9},{2,6},{3,7},{6... | collective-permute-start | bytes 196616 | tf_op jit(solution)/shard_map/ppermute | solution.py:26
  10.3 2.1 %collective-permute-start.3 = (bf16[224,128]{1,0:T(8,128)(2,1)S(1)}, bf16[224,128]{1,0:T(8,128)(2,1)S(1)}, u32[]{:S(2)}, u32[]{:S(2)}) collective-permute-start(bf16[224,128]{1,0:T(8,128)(2,1)S(1)} %get-tuple-element.19), channel_id=1, source_target_pairs={{0,13},{1,12},{4,9},{5,8},{8,5},{9,4},{12,1},{13,0},{2,15},{3,14},... | collective-permute-start | bytes 172040 | tf_op jit(solution)/shard_map/ppermute | solution.py:26
  12.4 0.0 collective-permute-done.5.refs_1_
  12.4 0.6 %shard_map.31 = (f32[480,128]{1,0:T(8,128)S(1)}, f32[480,256]{1,0:T(8,128)S(1)}) custom-call(bf16[480,128]{1,0:T(8,128)(2,1)S(1)} %get-tuple-element.16.refs_0_, bf16[480,128]{1,0:T(8,128)(2,1)S(1)} %collective-permute-done.5.refs_1_, bf16[480,128]{1,0:T(8,128)(2,1)S(1)} %get-tuple-element.18.refs_2_.refs_3_), custom_call_target="tpu_custom_call" | custom-call | flops 176947200 | bytes 122880 | tf_op jit(solution)/shard_map/pallas_call | solution.py:156
  13.0 0.6 %shard_map.32 = (f32[480,128]{1,0:T(8,128)S(1)}, f32[480,256]{1,0:T(8,128)S(1)}) custom-call(bf16[480,128]{1,0:T(8,128)(2,1)S(1)} %get-tuple-element.16.refs_0_, bf16[480,128]{1,0:T(8,128)(2,1)S(1)} %collective-permute-done.1.refs_1_, bf16[480,128]{1,0:T(8,128)(2,1)S(1)} %get-tuple-element.18.refs_2_.refs_3_, f32[480,128]{1,0:T(8,128)S(1)} %get-tuple-element.20.refs_3_, ...), custom_call_target="tpu_custom_call" | custom-call | flops 176947200 | bytes 122880 | tf_op jit(solution)/shard_map/pallas_call | solution.py:156
  13.7 0.0 collective-permute-done.4.refs_1_
  13.7 0.6 %shard_map.33 = (f32[480,128]{1,0:T(8,128)S(1)}, f32[480,256]{1,0:T(8,128)S(1)}) custom-call(bf16[480,128]{1,0:T(8,128)(2,1)S(1)} %get-tuple-element.16.refs_0_, bf16[480,128]{1,0:T(8,128)(2,1)S(1)} %collective-permute-done.4.refs_1_, bf16[480,128]{1,0:T(8,128)(2,1)S(1)} %get-tuple-element.18.refs_2_.refs_3_, f32[480,128]{1,0:T(8,128)S(1)} %get-tuple-element.22.refs_3_, ...), custom_call_target="tpu_custom_call" | custom-call | flops 176947200 | bytes 122880 | tf_op jit(solution)/shard_map/pallas_call | solution.py:156
  14.3 2.0 %collective-permute-done.3.refs_1_ = bf16[224,128]{1,0:T(8,128)(2,1)S(1)} collective-permute-done((bf16[224,128]{1,0:T(8,128)(2,1)S(1)}, bf16[224,128]{1,0:T(8,128)(2,1)S(1)}, u32[]{:S(2)}, u32[]{:S(2)}) %collective-permute-start.3) | collective-permute-done | bytes 57376 | tf_op jit(solution)/shard_map/ppermute | solution.py:26
  16.3 0.5 %shard_map.34 = (f32[480,128]{1,0:T(8,128)S(1)}, f32[480,256]{1,0:T(8,128)S(1)}) custom-call(bf16[480,128]{1,0:T(8,128)(2,1)S(1)} %get-tuple-element.16.refs_0_, bf16[224,128]{1,0:T(8,128)(2,1)S(1)} %collective-permute-done.3.refs_1_, bf16[480,128]{1,0:T(8,128)(2,1)S(1)} %get-tuple-element.18.refs_2_.refs_3_, f32[480,128]{1,0:T(8,128)S(1)} %get-tuple-element.24.refs_3_, ...), custom_call_target="tpu_custom_call" | custom-call | flops 82575360 | bytes 57344 | tf_op jit(solution)/shard_map/pallas_call | solution.py:156
  16.8 0.0 collective-permute-done.refs_1_
  16.8 0.0 collective-permute-done.2.refs_2_
  16.8 1.3 %shard_map.35 = (f32[2,480]{1,0:T(2,128)}, bf16[480,128]{1,0:T(8,128)(2,1)}) custom-call(bf16[480,128]{1,0:T(8,128)(2,1)S(1)} %get-tuple-element.16.refs_0_, bf16[256,128]{1,0:T(8,128)(2,1)S(1)} %collective-permute-done.refs_1_, bf16[256,128]{1,0:T(8,128)(2,1)S(1)} %collective-permute-done.2.refs_2_, bf16[480,128]{1,0:T(8,128)(2,1)S(1)} %get-tuple-element.18.refs_2_.refs_3_, ...), custom_call_target="tpu_custom_call" | custom-call | flops 94371840 | bytes 65536 | tf_op jit(solution)/shard_map/pallas_call | solution.py:156
  (1 shorter events, 0.0 us)
Async XLA Ops:
  0.6 7.6 %collective-permute-start.1 = (bf16[480,128]{1,0:T(8,128)(2,1)}, bf16[480,128]{1,0:T(8,128)(2,1)S(1)}, u32[]{:S(2)}, u32[]{:S(2)}) collective-permute-start(bf16[480,128]{1,0:T(8,128)(2,1)} %bitcast.3), channel_id=1, source_target_pairs={{0,9},{1,8},{4,1},{5,0},{8,13},{9,12},{12,5},{13,4},{2,11},{3,10},... | collective-permute-start | bytes 368648 | tf_op jit(solution)/shard_map/ppermute | solution.py:26
  4.2 8.2 %collective-permute-start.5 = (bf16[480,128]{1,0:T(8,128)(2,1)}, bf16[480,128]{1,0:T(8,128)(2,1)S(1)}, u32[]{:S(2)}, u32[]{:S(2)}) collective-permute-start(bf16[480,128]{1,0:T(8,128)(2,1)} %bitcast.4), channel_id=1, source_target_pairs={{0,1},{1,0},{4,5},{5,4},{8,9},{9,8},{12,13},{13,12},{2,3},{3,2},{6... | collective-permute-start | bytes 368648 | tf_op jit(solution)/shard_map/ppermute | solution.py:26
  4.9 8.8 %collective-permute-start.4 = (bf16[480,128]{1,0:T(8,128)(2,1)}, bf16[480,128]{1,0:T(8,128)(2,1)S(1)}, u32[]{:S(2)}, u32[]{:S(2)}) collective-permute-start(bf16[480,128]{1,0:T(8,128)(2,1)} %bitcast.5), channel_id=1, source_target_pairs={{0,5},{1,4},{4,13},{5,12},{8,1},{9,0},{12,9},{13,8},{2,7},{3,6},{6... | collective-permute-start | bytes 368648 | tf_op jit(solution)/shard_map/ppermute | solution.py:26
  4.9 0.9 %copy-start = (bf16[1,1,480,128]{3,2,1,0:T(8,128)(2,1)S(1)}, bf16[1,1,480,128]{3,2,1,0:T(8,128)(2,1)}, u32[]{:S(2)}) copy-start(bf16[1,1,480,128]{3,2,1,0:T(8,128)(2,1)} %param.1) | copy-start | bytes 368644
  5.9 10.9 %collective-permute-start = (bf16[256,128]{1,0:T(8,128)(2,1)S(1)}, bf16[256,128]{1,0:T(8,128)(2,1)S(1)}, u32[]{:S(2)}, u32[]{:S(2)}) collective-permute-start(bf16[256,128]{1,0:T(8,128)(2,1)S(1)} %get-tuple-element.17), channel_id=1, source_target_pairs={{0,1},{1,0},{4,9},{5,8},{8,5},{9,4},{12,13},{13,12},{2,3},{3,2},{6... | collective-permute-start | bytes 196616 | tf_op jit(solution)/shard_map/ppermute | solution.py:26
  8.3 8.6 %collective-permute-start.2 = (bf16[256,128]{1,0:T(8,128)(2,1)S(1)}, bf16[256,128]{1,0:T(8,128)(2,1)S(1)}, u32[]{:S(2)}, u32[]{:S(2)}) collective-permute-start(bf16[256,128]{1,0:T(8,128)(2,1)S(1)} %slice.4), channel_id=1, source_target_pairs={{0,4},{1,5},{4,0},{5,1},{8,12},{9,13},{12,8},{13,9},{2,6},{3,7},{6... | collective-permute-start | bytes 196616 | tf_op jit(solution)/shard_map/ppermute | solution.py:26
  10.3 6.0 %collective-permute-start.3 = (bf16[224,128]{1,0:T(8,128)(2,1)S(1)}, bf16[224,128]{1,0:T(8,128)(2,1)S(1)}, u32[]{:S(2)}, u32[]{:S(2)}) collective-permute-start(bf16[224,128]{1,0:T(8,128)(2,1)S(1)} %get-tuple-element.19), channel_id=1, source_target_pairs={{0,13},{1,12},{4,9},{5,8},{8,5},{9,4},{12,1},{13,0},{2,15},{3,14},... | collective-permute-start | bytes 172040 | tf_op jit(solution)/shard_map/ppermute | solution.py:26

commit v4 on v2

--- a/solution.py
+++ b/solution.py
@@ -57,7 +57,7 @@
 def fold_kernel(blocks, spans, first, last, *refs):
     refs = list(refs)
     q_ref = refs.pop(0)
-    key_refs = [[refs.pop(0) for _ in range(n)] for _, n in blocks]
+    key_refs = [[refs.pop(0) for _ in range(n)] for _, _, n in blocks]
     places_ref = refs.pop(0)
     if not first:
         top_in, acc_in = refs.pop(0), refs.pop(0)
@@ -66,14 +66,15 @@
     here = lax.axis_index("pix")
     column = lax.broadcasted_iota(jnp.int32, (1, chans), 1)
     keys, values = [], []
-    for (table, _), held in zip(blocks, key_refs):
+    for (table, begin, _), held in zip(blocks, key_refs):
         part = held[0][...]
         if len(held) > 1:
             part = jnp.where((here == 0) | (here == len(table) - 1), held[1][...], part)
-        start_row = pick(table) * (part.shape[0] // W)
+        start_row = pick(table) * (rows // W)
         offset = jnp.where(column == 1, start_row, 0).astype(jnp.float32).astype(jnp.bfloat16)
         keys.append(part)
-        values.append(jnp.concatenate([part, places_ref[...] + offset], axis=1))
+        place = places_ref[begin : begin + part.shape[0], :]
+        values.append(jnp.concatenate([part, place + offset], axis=1))
     keys = jnp.concatenate(keys, axis=0) if len(keys) > 1 else keys[0]
     values = jnp.concatenate(values, axis=0) if len(values) > 1 else values[0]
     count = keys.shape[0]
@@ -136,8 +137,8 @@
     first = carry is None
     middle = (rows // 2 + 127) // 128 * 128
     spans = [(0, middle), (middle, rows)] if middle < rows else [(0, rows)]
-    operands = [queries, *[part for _, held in blocks for part in held], positions, *(carry or ())]
-    keys = sum(held[0].shape[0] for _, held in blocks)
+    operands = [queries, *[part for _, _, held in blocks for part in held], positions, *(carry or ())]
+    keys = sum(held[0].shape[0] for _, _, held in blocks)
     if last:
         shapes = ((2, rows), jnp.float32), ((rows, chans), jnp.bfloat16)
         scratch = [pltpu.VMEM(shape, kind) for shape, kind in shapes]
@@ -146,7 +147,7 @@
         shapes = ((rows, chans), jnp.float32), ((rows, 2 * chans), jnp.float32)
         scratch = []
     return pl.pallas_call(
-        functools.partial(fold_kernel, [(table, len(held)) for table, held in blocks], spans, first, last),
+        functools.partial(fold_kernel, [(table, begin, len(held)) for table, begin, held in blocks], spans, first, last),
         out_shape=[jax.ShapeDtypeStruct(shape, kind) for shape, kind in shapes],
         in_specs=[VMEM] * len(operands),
         out_specs=[ANY if last else VMEM] * len(shapes),
@@ -165,7 +166,6 @@
 def body(features):
     rows, chans = features.shape[2:]
     pix = lax.axis_size("pix")
-    straight = list(range(pix))
     own = features.reshape(rows, chans)
 
     def send(array, targets, cross=True):
@@ -173,22 +173,16 @@
 
     positions = places(rows, chans)
     if pix == 4:
-        far = send(own, [2, 0, 3, 1])
-        back = send(own, [1, 3, 0, 2])
-        zero = send(own, straight)
-        mid = send(own, [0, 2, 1, 3])
-        relay = send(far, [1, 0, 3, 2], False)
-        groups = [
-            [(straight, [zero])],
-            [(sources_of([2, 0, 3, 1]), [far])],
-            [(sources_of([1, 3, 0, 2]), [back])],
-            [(straight[::-1], [mid, relay])],
-        ]
+        x0 = send(own, [2, 0, 1, 3])
+        x1 = send(own, [1, 2, 3, 0])
+        x2 = send(own, [0, 3, 2, 1])
+        relay = send(x0, [1, 0, 3, 2], False)
+        groups = [[(sources_of(t), 0, [x])] for t, x in (([2, 0, 1, 3], x0), ([1, 2, 3, 0], x1), ([0, 3, 2, 1], x2), ([3, 1, 0, 2], relay))]
     else:
         groups = []
         for shift in range(pix):
             targets = [(z + shift) % pix for z in range(pix)]
-            groups.append([(sources_of(targets), [send(own, targets)])])
+            groups.append([(sources_of(targets), 0, [send(own, targets)])])
     carry = None
     for place, blocks in enumerate(groups):
         carry = fold(own, positions, blocks, carry, place == len(groups) - 1)

time: 16.8 us -> 16.1 us (0.958)
  starting transfers between devices: 6.26 us -> 5.4 us
    ppermute x5 -> x4, starting transfers between devices: 6.26 us -> 5.4 us  [hop(): return lax.ppermute(array, ('pix', 'dir'), pairs)]
    ppermute x5 -> x4, waiting for transfers between devices: 6.31 us -> 6.45 us  [hop(): return lax.ppermute(array, ('pix', 'dir'), pairs)]
  transfers between devices with their start and end apart: 5 -> 4, of which waited for: 3 -> 3; matrix products, arithmetic and copies ran while one was open for 0% -> 0% of each run, Pallas kernels for 12% -> 12%
where the time goes in v4:
time: 16.1 us; the launch traced here: 15.9 us
  waiting for transfers between devices  6.45 us (40%)
  starting transfers between devices  5.4 us (34%)
  Pallas kernels  3.38 us (21%)
  between operations  0.68 us (4%)
    ppermute x4, waiting for transfers between devices, hop(): return lax.ppermute(array, ('pix', 'dir'), pairs)  6.45 us
    ppermute x4, starting transfers between devices, hop(): return lax.ppermute(array, ('pix', 'dir'), pairs)  5.4 us
    pallas_call x4, Pallas kernels, fold(): pl.pallas_call(functools.partial(fold_kernel, [(table, begin, len(held))...  3.29 us
  transfers between devices with their start and end apart: 4, of which 3 were waited for; matrix products, arithmetic and copies ran while one was open for 0% of the time, Pallas kernels for 12%

profile of v4, /device:TPU:0, one launch (start us, length us, event | category | flops | bytes accessed | tf_op | source)
XLA Modules:
  0.0 15.9 jit_solution(260517473365522850)
XLA Ops:
  0.6 0.0 copy-start
  0.6 3.6 %collective-permute-start = (bf16[480,128]{1,0:T(8,128)(2,1)}, bf16[480,128]{1,0:T(8,128)(2,1)S(1)}, u32[]{:S(2)}, u32[]{:S(2)}) collective-permute-start(bf16[480,128]{1,0:T(8,128)(2,1)} %bitcast.3), channel_id=1, source_target_pairs={{0,9},{1,8},{4,1},{5,0},{8,5},{9,4},{12,13},{13,12},{2,11},{3,10},... | collective-permute-start | bytes 368648 | tf_op jit(solution)/shard_map/ppermute | solution.py:26
  4.2 0.0 collective-permute-start.3
  4.2 0.7 %collective-permute-start.2 = (bf16[480,128]{1,0:T(8,128)(2,1)}, bf16[480,128]{1,0:T(8,128)(2,1)S(1)}, u32[]{:S(2)}, u32[]{:S(2)}) collective-permute-start(bf16[480,128]{1,0:T(8,128)(2,1)} %bitcast.5), channel_id=1, source_target_pairs={{0,1},{1,0},{4,13},{5,12},{8,9},{9,8},{12,5},{13,4},{2,3},{3,2},{6... | collective-permute-start | bytes 368648 | tf_op jit(solution)/shard_map/ppermute | solution.py:26
  4.9 3.4 %collective-permute-done.refs_1_ = bf16[480,128]{1,0:T(8,128)(2,1)S(1)} collective-permute-done((bf16[480,128]{1,0:T(8,128)(2,1)}, bf16[480,128]{1,0:T(8,128)(2,1)S(1)}, u32[]{:S(2)}, u32[]{:S(2)}) %collective-permute-start) | collective-permute-done | bytes 122912 | tf_op jit(solution)/shard_map/ppermute | solution.py:26
  8.3 1.2 %collective-permute-start.1 = (bf16[480,128]{1,0:T(8,128)(2,1)S(1)}, bf16[480,128]{1,0:T(8,128)(2,1)S(1)}, u32[]{:S(2)}, u32[]{:S(2)}) collective-permute-start(bf16[480,128]{1,0:T(8,128)(2,1)S(1)} %collective-permute-done.refs_1_), channel_id=1, source_target_pairs={{0,4},{1,5},{4,0},{5,1},{8,12},{9,13},{12,8},{13,9},{2,6},{3,7},{6... | collective-permute-start | bytes 368648 | tf_op jit(solution)/shard_map/ppermute | solution.py:26
  9.4 0.1 shard_map.30.refs_2_
  9.5 0.0 copy-done
  9.5 0.6 %shard_map.31 = (f32[480,128]{1,0:T(8,128)S(1)}, f32[480,256]{1,0:T(8,128)S(1)}) custom-call(bf16[480,128]{1,0:T(8,128)(2,1)S(1)} %bitcast.6, bf16[480,128]{1,0:T(8,128)(2,1)S(1)} %collective-permute-done.refs_1_, bf16[480,128]{1,0:T(8,128)(2,1)S(1)} %shard_map.30.refs_2_), custom_call_target="tpu_custom_call" | custom-call | flops 176947200 | bytes 122880 | tf_op jit(solution)/shard_map/pallas_call | solution.py:149
  10.2 0.8 %collective-permute-done.3.refs_1_ = bf16[480,128]{1,0:T(8,128)(2,1)S(1)} collective-permute-done((bf16[480,128]{1,0:T(8,128)(2,1)}, bf16[480,128]{1,0:T(8,128)(2,1)S(1)}, u32[]{:S(2)}, u32[]{:S(2)}) %collective-permute-start.3) | collective-permute-done | bytes 122912 | tf_op jit(solution)/shard_map/ppermute | solution.py:26
  11.0 0.6 %shard_map.32 = (f32[480,128]{1,0:T(8,128)S(1)}, f32[480,256]{1,0:T(8,128)S(1)}) custom-call(bf16[480,128]{1,0:T(8,128)(2,1)S(1)} %bitcast.7, bf16[480,128]{1,0:T(8,128)(2,1)S(1)} %collective-permute-done.3.refs_1_, bf16[480,128]{1,0:T(8,128)(2,1)S(1)} %shard_map.30.refs_2_, f32[480,128]{1,0:T(8,128)S(1)} %get-tuple-element.10.refs_3_, ...), custom_call_target="tpu_custom_call" | custom-call | flops 176947200 | bytes 122880 | tf_op jit(solution)/shard_map/pallas_call | solution.py:149
  11.6 0.0 collective-permute-done.2.refs_1_
  11.6 0.6 %shard_map.33 = (f32[480,128]{1,0:T(8,128)S(1)}, f32[480,256]{1,0:T(8,128)S(1)}) custom-call(bf16[480,128]{1,0:T(8,128)(2,1)S(1)} %bitcast.8, bf16[480,128]{1,0:T(8,128)(2,1)S(1)} %collective-permute-done.2.refs_1_, bf16[480,128]{1,0:T(8,128)(2,1)S(1)} %shard_map.30.refs_2_, f32[480,128]{1,0:T(8,128)S(1)} %get-tuple-element.12.refs_3_, ...), custom_call_target="tpu_custom_call" | custom-call | flops 176947200 | bytes 122880 | tf_op jit(solution)/shard_map/pallas_call | solution.py:149
  12.2 2.3 %collective-permute-done.1.refs_1_ = bf16[480,128]{1,0:T(8,128)(2,1)S(1)} collective-permute-done((bf16[480,128]{1,0:T(8,128)(2,1)S(1)}, bf16[480,128]{1,0:T(8,128)(2,1)S(1)}, u32[]{:S(2)}, u32[]{:S(2)}) %collective-permute-start.1) | collective-permute-done | bytes 122912 | tf_op jit(solution)/shard_map/ppermute | solution.py:26
  14.5 1.5 %shard_map.34 = (f32[2,480]{1,0:T(2,128)}, bf16[480,128]{1,0:T(8,128)(2,1)}) custom-call(bf16[480,128]{1,0:T(8,128)(2,1)S(1)} %bitcast.9, bf16[480,128]{1,0:T(8,128)(2,1)S(1)} %collective-permute-done.1.refs_1_, bf16[480,128]{1,0:T(8,128)(2,1)S(1)} %shard_map.30.refs_2_, f32[480,128]{1,0:T(8,128)S(1)} %get-tuple-element.14.refs_3_, ...), custom_call_target="tpu_custom_call" | custom-call | flops 176947200 | bytes 122880 | tf_op jit(solution)/shard_map/pallas_call | solution.py:149
Async XLA Ops:
  0.6 8.9 %copy-start = (bf16[1,1,480,128]{3,2,1,0:T(8,128)(2,1)S(1)}, bf16[1,1,480,128]{3,2,1,0:T(8,128)(2,1)}, u32[]{:S(2)}) copy-start(bf16[1,1,480,128]{3,2,1,0:T(8,128)(2,1)} %param.1) | copy-start | bytes 368644
  0.6 7.6 %collective-permute-start = (bf16[480,128]{1,0:T(8,128)(2,1)}, bf16[480,128]{1,0:T(8,128)(2,1)S(1)}, u32[]{:S(2)}, u32[]{:S(2)}) collective-permute-start(bf16[480,128]{1,0:T(8,128)(2,1)} %bitcast.3), channel_id=1, source_target_pairs={{0,9},{1,8},{4,1},{5,0},{8,5},{9,4},{12,13},{13,12},{2,11},{3,10},... | collective-permute-start | bytes 368648 | tf_op jit(solution)/shard_map/ppermute | solution.py:26
  4.2 6.8 %collective-permute-start.3 = (bf16[480,128]{1,0:T(8,128)(2,1)}, bf16[480,128]{1,0:T(8,128)(2,1)S(1)}, u32[]{:S(2)}, u32[]{:S(2)}) collective-permute-start(bf16[480,128]{1,0:T(8,128)(2,1)} %bitcast.4), channel_id=1, source_target_pairs={{0,5},{1,4},{4,9},{5,8},{8,13},{9,12},{12,1},{13,0},{2,7},{3,6},{6... | collective-permute-start | bytes 368648 | tf_op jit(solution)/shard_map/ppermute | solution.py:26
  4.2 7.4 %collective-permute-start.2 = (bf16[480,128]{1,0:T(8,128)(2,1)}, bf16[480,128]{1,0:T(8,128)(2,1)S(1)}, u32[]{:S(2)}, u32[]{:S(2)}) collective-permute-start(bf16[480,128]{1,0:T(8,128)(2,1)} %bitcast.5), channel_id=1, source_target_pairs={{0,1},{1,0},{4,13},{5,12},{8,9},{9,8},{12,5},{13,4},{2,3},{3,2},{6... | collective-permute-start | bytes 368648 | tf_op jit(solution)/shard_map/ppermute | solution.py:26
  8.3 6.2 %collective-permute-start.1 = (bf16[480,128]{1,0:T(8,128)(2,1)S(1)}, bf16[480,128]{1,0:T(8,128)(2,1)S(1)}, u32[]{:S(2)}, u32[]{:S(2)}) collective-permute-start(bf16[480,128]{1,0:T(8,128)(2,1)S(1)} %collective-permute-done.refs_1_), channel_id=1, source_target_pairs={{0,4},{1,5},{4,0},{5,1},{8,12},{9,13},{12,8},{13,9},{2,6},{3,7},{6... | collective-permute-start | bytes 368648 | tf_op jit(solution)/shard_map/ppermute | solution.py:26

commit v5 on v4

--- a/solution.py
+++ b/solution.py
@@ -120,7 +120,8 @@
             )
         )
         copies[-1].start()
-        sums = jnp.transpose(acc[:, chans:] * inverse)[:2, :]
+        sums = jnp.transpose(acc[:, chans : chans + 8])
+        sums = sums[:2, :] / sums[2:3, :]
         index = here * rows + begin + lax.broadcasted_iota(jnp.int32, (1, end - begin), 1)
         index = index.astype(jnp.float32)
         own_row = jnp.floor((index + 0.5) * (1.0 / W))
@@ -135,8 +136,8 @@
 def fold(queries, positions, blocks, carry, last):
     rows, chans = queries.shape
     first = carry is None
-    middle = (rows // 2 + 127) // 128 * 128
-    spans = [(0, middle), (middle, rows)] if middle < rows else [(0, rows)]
+    step = 128 if last else (rows // 2 + 127) // 128 * 128
+    spans = [(begin, min(begin + step, rows)) for begin in range(0, rows, step)]
     operands = [queries, *[part for _, _, held in blocks for part in held], positions, *(carry or ())]
     keys = sum(held[0].shape[0] for _, _, held in blocks)
     if last:
@@ -173,11 +174,19 @@
 
     positions = places(rows, chans)
     if pix == 4:
+        cut = rows * 7 // 240 * 16
         x0 = send(own, [2, 0, 1, 3])
         x1 = send(own, [1, 2, 3, 0])
         x2 = send(own, [0, 3, 2, 1])
-        relay = send(x0, [1, 0, 3, 2], False)
-        groups = [[(sources_of(t), 0, [x])] for t, x in (([2, 0, 1, 3], x0), ([1, 2, 3, 0], x1), ([0, 3, 2, 1], x2), ([3, 1, 0, 2], relay))]
+        relaya = send(x0[:cut], [1, 0, 3, 2], False)
+        relayb = send(x0[cut:], [1, 0, 3, 2], False)
+        groups = [
+            [([1, 2, 0, 3], 0, [x0])],
+            [([3, 0, 1, 2], 0, [x1])],
+            [([0, 3, 2, 1], 0, [x2])],
+            [([2, 1, 3, 0], 0, [relaya])],
+            [([2, 1, 3, 0], cut, [relayb])],
+        ]
     else:
         groups = []
         for shift in range(pix):

time: 16.1 us -> 16.4 us (1.019)
  waiting for transfers between devices: 6.45 us -> 5.59 us
  starting transfers between devices: 5.4 us -> 6.26 us
  Pallas kernels: 3.38 us -> 3.64 us
    ppermute x4 -> x5, waiting for transfers between devices: 6.45 us -> 5.59 us  [hop(): return lax.ppermute(array, ('pix', 'dir'), pairs)]
    ppermute x4 -> x5, starting transfers between devices: 5.4 us -> 6.26 us  [hop(): return lax.ppermute(array, ('pix', 'dir'), pairs)]
    pallas_call x4 -> x5, Pallas kernels: 3.29 us -> 3.55 us  [fold(): pl.pallas_call(functools.partial(fold_kernel, [(table, begin, len(held))...]
  transfers between devices with their start and end apart: 4 -> 5, of which waited for: 3 -> 2; matrix products, arithmetic and copies ran while one was open for 0% -> 0% of each run, Pallas kernels for 12% -> 15%
where the time goes in v5:
time: 16.4 us; the launch traced here: 16.2 us
  starting transfers between devices  6.26 us (38%)
  waiting for transfers between devices  5.59 us (34%)
  Pallas kernels  3.64 us (22%)
  between operations  0.7 us (4%)
    ppermute x5, starting transfers between devices, hop(): return lax.ppermute(array, ('pix', 'dir'), pairs)  6.26 us
    ppermute x5, waiting for transfers between devices, hop(): return lax.ppermute(array, ('pix', 'dir'), pairs)  5.59 us
    pallas_call x5, Pallas kernels, fold(): pl.pallas_call(functools.partial(fold_kernel, [(table, begin, len(held))...  3.55 us
  transfers between devices with their start and end apart: 5, of which 2 were waited for; matrix products, arithmetic and copies ran while one was open for 0% of the time, Pallas kernels for 15%

profile of v5, /device:TPU:0, one launch (start us, length us, event | category | flops | bytes accessed | tf_op | source)
XLA Modules:
  0.0 16.2 jit_solution(14274675731345619806)
XLA Ops:
  0.6 3.6 %collective-permute-start = (bf16[480,128]{1,0:T(8,128)(2,1)}, bf16[480,128]{1,0:T(8,128)(2,1)S(1)}, u32[]{:S(2)}, u32[]{:S(2)}) collective-permute-start(bf16[480,128]{1,0:T(8,128)(2,1)} %bitcast.3), channel_id=1, source_target_pairs={{0,9},{1,8},{4,1},{5,0},{8,5},{9,4},{12,13},{13,12},{2,11},{3,10},... | collective-permute-start | bytes 368648 | tf_op jit(solution)/shard_map/ppermute | solution.py:26
  4.2 0.0 collective-permute-start.4
  4.2 0.7 %collective-permute-start.3 = (bf16[480,128]{1,0:T(8,128)(2,1)}, bf16[480,128]{1,0:T(8,128)(2,1)S(1)}, u32[]{:S(2)}, u32[]{:S(2)}) collective-permute-start(bf16[480,128]{1,0:T(8,128)(2,1)} %bitcast.5), channel_id=1, source_target_pairs={{0,1},{1,0},{4,13},{5,12},{8,9},{9,8},{12,5},{13,4},{2,3},{3,2},{6... | collective-permute-start | bytes 368648 | tf_op jit(solution)/shard_map/ppermute | solution.py:26
  4.9 3.4 %collective-permute-done.refs_1_ = bf16[480,128]{1,0:T(8,128)(2,1)S(1)} collective-permute-done((bf16[480,128]{1,0:T(8,128)(2,1)}, bf16[480,128]{1,0:T(8,128)(2,1)S(1)}, u32[]{:S(2)}, u32[]{:S(2)}) %collective-permute-start) | collective-permute-done | bytes 122912 | tf_op jit(solution)/shard_map/ppermute | solution.py:26
  8.3 0.0 copy-start
  8.3 1.2 %collective-permute-start.1 = (bf16[256,128]{1,0:T(8,128)(2,1)S(1)}, bf16[256,128]{1,0:T(8,128)(2,1)S(1)}, u32[]{:S(2)}, u32[]{:S(2)}) collective-permute-start(bf16[256,128]{1,0:T(8,128)(2,1)S(1)} %slice.8), channel_id=1, source_target_pairs={{0,4},{1,5},{4,0},{5,1},{8,12},{9,13},{12,8},{13,9},{2,6},{3,7},{6... | collective-permute-start | bytes 196616 | tf_op jit(solution)/shard_map/ppermute | solution.py:26
  9.5 0.8 %collective-permute-start.2 = (bf16[224,128]{1,0:T(8,128)(2,1)S(1)}, bf16[224,128]{1,0:T(8,128)(2,1)S(1)}, u32[]{:S(2)}, u32[]{:S(2)}) collective-permute-start(bf16[224,128]{1,0:T(8,128)(2,1)S(1)} %slice.9), channel_id=1, source_target_pairs={{0,4},{1,5},{4,0},{5,1},{8,12},{9,13},{12,8},{13,9},{2,6},{3,7},{6... | collective-permute-start | bytes 172040 | tf_op jit(solution)/shard_map/ppermute | solution.py:26
  10.3 0.1 shard_map.30.refs_2_
  10.4 0.0 copy-done
  10.4 0.6 %shard_map.31 = (f32[480,128]{1,0:T(8,128)S(1)}, f32[480,256]{1,0:T(8,128)S(1)}) custom-call(bf16[480,128]{1,0:T(8,128)(2,1)S(1)} %bitcast.6, bf16[480,128]{1,0:T(8,128)(2,1)S(1)} %collective-permute-done.refs_1_, bf16[480,128]{1,0:T(8,128)(2,1)S(1)} %shard_map.30.refs_2_), custom_call_target="tpu_custom_call" | custom-call | flops 176947200 | bytes 122880 | tf_op jit(solution)/shard_map/pallas_call | solution.py:150
  11.0 0.0 collective-permute-done.4.refs_1_
  11.0 0.6 %shard_map.32 = (f32[480,128]{1,0:T(8,128)S(1)}, f32[480,256]{1,0:T(8,128)S(1)}) custom-call(bf16[480,128]{1,0:T(8,128)(2,1)S(1)} %bitcast.7, bf16[480,128]{1,0:T(8,128)(2,1)S(1)} %collective-permute-done.4.refs_1_, bf16[480,128]{1,0:T(8,128)(2,1)S(1)} %shard_map.30.refs_2_, f32[480,128]{1,0:T(8,128)S(1)} %get-tuple-element.12.refs_3_, ...), custom_call_target="tpu_custom_call" | custom-call | flops 176947200 | bytes 122880 | tf_op jit(solution)/shard_map/pallas_call | solution.py:150
  11.6 0.0 collective-permute-done.3.refs_1_
  11.6 0.6 %shard_map.33 = (f32[480,128]{1,0:T(8,128)S(1)}, f32[480,256]{1,0:T(8,128)S(1)}) custom-call(bf16[480,128]{1,0:T(8,128)(2,1)S(1)} %bitcast.8, bf16[480,128]{1,0:T(8,128)(2,1)S(1)} %collective-permute-done.3.refs_1_, bf16[480,128]{1,0:T(8,128)(2,1)S(1)} %shard_map.30.refs_2_, f32[480,128]{1,0:T(8,128)S(1)} %get-tuple-element.14.refs_3_, ...), custom_call_target="tpu_custom_call" | custom-call | flops 176947200 | bytes 122880 | tf_op jit(solution)/shard_map/pallas_call | solution.py:150
  12.3 2.2 %collective-permute-done.2.refs_1_ = bf16[224,128]{1,0:T(8,128)(2,1)S(1)} collective-permute-done((bf16[224,128]{1,0:T(8,128)(2,1)S(1)}, bf16[224,128]{1,0:T(8,128)(2,1)S(1)}, u32[]{:S(2)}, u32[]{:S(2)}) %collective-permute-start.2) | collective-permute-done | bytes 57376 | tf_op jit(solution)/shard_map/ppermute | solution.py:26
  14.4 0.5 %shard_map.34 = (f32[480,128]{1,0:T(8,128)S(1)}, f32[480,256]{1,0:T(8,128)S(1)}) custom-call(bf16[480,128]{1,0:T(8,128)(2,1)S(1)} %bitcast.9, bf16[224,128]{1,0:T(8,128)(2,1)S(1)} %collective-permute-done.2.refs_1_, bf16[480,128]{1,0:T(8,128)(2,1)S(1)} %shard_map.30.refs_2_, f32[480,128]{1,0:T(8,128)S(1)} %get-tuple-element.16.refs_3_, ...), custom_call_target="tpu_custom_call" | custom-call | flops 82575360 | bytes 57344 | tf_op jit(solution)/shard_map/pallas_call | solution.py:150
  14.9 0.0 collective-permute-done.1.refs_1_
  14.9 1.3 %shard_map.35 = (f32[2,480]{1,0:T(2,128)}, bf16[480,128]{1,0:T(8,128)(2,1)}) custom-call(bf16[480,128]{1,0:T(8,128)(2,1)S(1)} %bitcast.10, bf16[256,128]{1,0:T(8,128)(2,1)S(1)} %collective-permute-done.1.refs_1_, bf16[480,128]{1,0:T(8,128)(2,1)S(1)} %shard_map.30.refs_2_, f32[480,128]{1,0:T(8,128)S(1)} %get-tuple-element.18.refs_3_, ...), custom_call_target="tpu_custom_call" | custom-call | flops 94371840 | bytes 65536 | tf_op jit(solution)/shard_map/pallas_call | solution.py:150
  (2 shorter events, 0.0 us)
Async XLA Ops:
  0.6 7.6 %collective-permute-start = (bf16[480,128]{1,0:T(8,128)(2,1)}, bf16[480,128]{1,0:T(8,128)(2,1)S(1)}, u32[]{:S(2)}, u32[]{:S(2)}) collective-permute-start(bf16[480,128]{1,0:T(8,128)(2,1)} %bitcast.3), channel_id=1, source_target_pairs={{0,9},{1,8},{4,1},{5,0},{8,5},{9,4},{12,13},{13,12},{2,11},{3,10},... | collective-permute-start | bytes 368648 | tf_op jit(solution)/shard_map/ppermute | solution.py:26
  4.2 6.8 %collective-permute-start.4 = (bf16[480,128]{1,0:T(8,128)(2,1)}, bf16[480,128]{1,0:T(8,128)(2,1)S(1)}, u32[]{:S(2)}, u32[]{:S(2)}) collective-permute-start(bf16[480,128]{1,0:T(8,128)(2,1)} %bitcast.4), channel_id=1, source_target_pairs={{0,5},{1,4},{4,9},{5,8},{8,13},{9,12},{12,1},{13,0},{2,7},{3,6},{6... | collective-permute-start | bytes 368648 | tf_op jit(solution)/shard_map/ppermute | solution.py:26
  4.2 7.5 %collective-permute-start.3 = (bf16[480,128]{1,0:T(8,128)(2,1)}, bf16[480,128]{1,0:T(8,128)(2,1)S(1)}, u32[]{:S(2)}, u32[]{:S(2)}) collective-permute-start(bf16[480,128]{1,0:T(8,128)(2,1)} %bitcast.5), channel_id=1, source_target_pairs={{0,1},{1,0},{4,13},{5,12},{8,9},{9,8},{12,5},{13,4},{2,3},{3,2},{6... | collective-permute-start | bytes 368648 | tf_op jit(solution)/shard_map/ppermute | solution.py:26
  8.3 2.1 %copy-start = (bf16[1,1,480,128]{3,2,1,0:T(8,128)(2,1)S(1)}, bf16[1,1,480,128]{3,2,1,0:T(8,128)(2,1)}, u32[]{:S(2)}) copy-start(bf16[1,1,480,128]{3,2,1,0:T(8,128)(2,1)} %param.1) | copy-start | bytes 368644
  8.3 6.7 %collective-permute-start.1 = (bf16[256,128]{1,0:T(8,128)(2,1)S(1)}, bf16[256,128]{1,0:T(8,128)(2,1)S(1)}, u32[]{:S(2)}, u32[]{:S(2)}) collective-permute-start(bf16[256,128]{1,0:T(8,128)(2,1)S(1)} %slice.8), channel_id=1, source_target_pairs={{0,4},{1,5},{4,0},{5,1},{8,12},{9,13},{12,8},{13,9},{2,6},{3,7},{6... | collective-permute-start | bytes 196616 | tf_op jit(solution)/shard_map/ppermute | solution.py:26
  9.5 4.9 %collective-permute-start.2 = (bf16[224,128]{1,0:T(8,128)(2,1)S(1)}, bf16[224,128]{1,0:T(8,128)(2,1)S(1)}, u32[]{:S(2)}, u32[]{:S(2)}) collective-permute-start(bf16[224,128]{1,0:T(8,128)(2,1)S(1)} %slice.9), channel_id=1, source_target_pairs={{0,4},{1,5},{4,0},{5,1},{8,12},{9,13},{12,8},{13,9},{2,6},{3,7},{6... | collective-permute-start | bytes 172040 | tf_op jit(solution)/shard_map/ppermute | solution.py:26

commit v6 on v5

--- a/solution.py
+++ b/solution.py
@@ -120,8 +120,7 @@
             )
         )
         copies[-1].start()
-        sums = jnp.transpose(acc[:, chans : chans + 8])
-        sums = sums[:2, :] / sums[2:3, :]
+        sums = jnp.transpose(acc[:, chans:] * inverse)[:2, :]
         index = here * rows + begin + lax.broadcasted_iota(jnp.int32, (1, end - begin), 1)
         index = index.astype(jnp.float32)
         own_row = jnp.floor((index + 0.5) * (1.0 / W))
@@ -174,7 +173,7 @@
 
     positions = places(rows, chans)
     if pix == 4:
-        cut = rows * 7 // 240 * 16
+        cut = rows * 8 // 240 * 16
         x0 = send(own, [2, 0, 1, 3])
         x1 = send(own, [1, 2, 3, 0])
         x2 = send(own, [0, 3, 2, 1])

time: 16.4 us -> 15.9 us (0.970)
  waiting for transfers between devices: 5.59 us -> 5.05 us
    ppermute x5, waiting for transfers between devices: 5.59 us -> 5.05 us  [hop(): return lax.ppermute(array, ('pix', 'dir'), pairs)]
  transfers between devices with their start and end apart: 5 -> 5, of which waited for: 2 -> 3; matrix products, arithmetic and copies ran while one was open for 0% -> 0% of each run, Pallas kernels for 15% -> 15%
where the time goes in v6:
time: 15.9 us; the launch traced here: 15.7 us
  starting transfers between devices  6.32 us (40%)
  waiting for transfers between devices  5.05 us (32%)
  Pallas kernels  3.65 us (23%)
  between operations  0.69 us (4%)
    ppermute x5, starting transfers between devices, hop(): return lax.ppermute(array, ('pix', 'dir'), pairs)  6.32 us
    ppermute x5, waiting for transfers between devices, hop(): return lax.ppermute(array, ('pix', 'dir'), pairs)  5.05 us
    pallas_call x5, Pallas kernels, fold(): pl.pallas_call(functools.partial(fold_kernel, [(table, begin, len(held))...  3.56 us
  transfers between devices with their start and end apart: 5, of which 3 were waited for; matrix products, arithmetic and copies ran while one was open for 0% of the time, Pallas kernels for 15%

profile of v6, /device:TPU:0, one launch (start us, length us, event | category | flops | bytes accessed | tf_op | source)
XLA Modules:
  0.0 15.7 jit_solution(1875429531324890772)
XLA Ops:
  0.6 3.6 %collective-permute-start = (bf16[480,128]{1,0:T(8,128)(2,1)}, bf16[480,128]{1,0:T(8,128)(2,1)S(1)}, u32[]{:S(2)}, u32[]{:S(2)}) collective-permute-start(bf16[480,128]{1,0:T(8,128)(2,1)} %bitcast.3), channel_id=1, source_target_pairs={{0,9},{1,8},{4,1},{5,0},{8,5},{9,4},{12,13},{13,12},{2,11},{3,10},... | collective-permute-start | bytes 368648 | tf_op jit(solution)/shard_map/ppermute | solution.py:26
  4.2 0.0 collective-permute-start.4
  4.2 0.7 %collective-permute-start.3 = (bf16[480,128]{1,0:T(8,128)(2,1)}, bf16[480,128]{1,0:T(8,128)(2,1)S(1)}, u32[]{:S(2)}, u32[]{:S(2)}) collective-permute-start(bf16[480,128]{1,0:T(8,128)(2,1)} %bitcast.5), channel_id=1, source_target_pairs={{0,1},{1,0},{4,13},{5,12},{8,9},{9,8},{12,5},{13,4},{2,3},{3,2},{6... | collective-permute-start | bytes 368648 | tf_op jit(solution)/shard_map/ppermute | solution.py:26
  4.9 3.4 %collective-permute-done.refs_1_ = bf16[480,128]{1,0:T(8,128)(2,1)S(1)} collective-permute-done((bf16[480,128]{1,0:T(8,128)(2,1)}, bf16[480,128]{1,0:T(8,128)(2,1)S(1)}, u32[]{:S(2)}, u32[]{:S(2)}) %collective-permute-start) | collective-permute-done | bytes 122912 | tf_op jit(solution)/shard_map/ppermute | solution.py:26
  8.3 0.0 copy-start
  8.3 1.2 %collective-permute-start.2 = (bf16[256,128]{1,0:T(8,128)(2,1)S(1)}, bf16[256,128]{1,0:T(8,128)(2,1)S(1)}, u32[]{:S(2)}, u32[]{:S(2)}) collective-permute-start(bf16[256,128]{1,0:T(8,128)(2,1)S(1)} %slice.9), channel_id=1, source_target_pairs={{0,4},{1,5},{4,0},{5,1},{8,12},{9,13},{12,8},{13,9},{2,6},{3,7},{6... | collective-permute-start | bytes 196616 | tf_op jit(solution)/shard_map/ppermute | solution.py:26
  9.5 0.1 shard_map.30.refs_2_
  9.6 0.8 %collective-permute-start.1 = (bf16[224,128]{1,0:T(8,128)(2,1)S(1)}, bf16[224,128]{1,0:T(8,128)(2,1)S(1)}, u32[]{:S(2)}, u32[]{:S(2)}) collective-permute-start(bf16[224,128]{1,0:T(8,128)(2,1)S(1)} %slice.8), channel_id=1, source_target_pairs={{0,4},{1,5},{4,0},{5,1},{8,12},{9,13},{12,8},{13,9},{2,6},{3,7},{6... | collective-permute-start | bytes 172040 | tf_op jit(solution)/shard_map/ppermute | solution.py:26
  10.5 0.0 copy-done
  10.5 0.6 %shard_map.31 = (f32[480,128]{1,0:T(8,128)S(1)}, f32[480,256]{1,0:T(8,128)S(1)}) custom-call(bf16[480,128]{1,0:T(8,128)(2,1)S(1)} %bitcast.6, bf16[480,128]{1,0:T(8,128)(2,1)S(1)} %collective-permute-done.refs_1_, bf16[480,128]{1,0:T(8,128)(2,1)S(1)} %shard_map.30.refs_2_), custom_call_target="tpu_custom_call" | custom-call | flops 176947200 | bytes 122880 | tf_op jit(solution)/shard_map/pallas_call | solution.py:149
  11.1 0.0 collective-permute-done.4.refs_1_
  11.1 0.6 %shard_map.32 = (f32[480,128]{1,0:T(8,128)S(1)}, f32[480,256]{1,0:T(8,128)S(1)}) custom-call(bf16[480,128]{1,0:T(8,128)(2,1)S(1)} %bitcast.7, bf16[480,128]{1,0:T(8,128)(2,1)S(1)} %collective-permute-done.4.refs_1_, bf16[480,128]{1,0:T(8,128)(2,1)S(1)} %shard_map.30.refs_2_, f32[480,128]{1,0:T(8,128)S(1)} %get-tuple-element.12.refs_3_, ...), custom_call_target="tpu_custom_call" | custom-call | flops 176947200 | bytes 122880 | tf_op jit(solution)/shard_map/pallas_call | solution.py:149
  11.7 0.0 collective-permute-done.3.refs_1_
  11.7 0.6 %shard_map.33 = (f32[480,128]{1,0:T(8,128)S(1)}, f32[480,256]{1,0:T(8,128)S(1)}) custom-call(bf16[480,128]{1,0:T(8,128)(2,1)S(1)} %bitcast.8, bf16[480,128]{1,0:T(8,128)(2,1)S(1)} %collective-permute-done.3.refs_1_, bf16[480,128]{1,0:T(8,128)(2,1)S(1)} %shard_map.30.refs_2_, f32[480,128]{1,0:T(8,128)S(1)} %get-tuple-element.14.refs_3_, ...), custom_call_target="tpu_custom_call" | custom-call | flops 176947200 | bytes 122880 | tf_op jit(solution)/shard_map/pallas_call | solution.py:149
  12.3 1.3 %collective-permute-done.2.refs_1_ = bf16[256,128]{1,0:T(8,128)(2,1)S(1)} collective-permute-done((bf16[256,128]{1,0:T(8,128)(2,1)S(1)}, bf16[256,128]{1,0:T(8,128)(2,1)S(1)}, u32[]{:S(2)}, u32[]{:S(2)}) %collective-permute-start.2) | collective-permute-done | bytes 65568 | tf_op jit(solution)/shard_map/ppermute | solution.py:26
  13.6 0.5 %shard_map.34 = (f32[480,128]{1,0:T(8,128)S(1)}, f32[480,256]{1,0:T(8,128)S(1)}) custom-call(bf16[480,128]{1,0:T(8,128)(2,1)S(1)} %bitcast.9, bf16[256,128]{1,0:T(8,128)(2,1)S(1)} %collective-permute-done.2.refs_1_, bf16[480,128]{1,0:T(8,128)(2,1)S(1)} %shard_map.30.refs_2_, f32[480,128]{1,0:T(8,128)S(1)} %get-tuple-element.16.refs_3_, ...), custom_call_target="tpu_custom_call" | custom-call | flops 94371840 | bytes 65536 | tf_op jit(solution)/shard_map/pallas_call | solution.py:149
  14.1 0.3 %collective-permute-done.1.refs_1_ = bf16[224,128]{1,0:T(8,128)(2,1)S(1)} collective-permute-done((bf16[224,128]{1,0:T(8,128)(2,1)S(1)}, bf16[224,128]{1,0:T(8,128)(2,1)S(1)}, u32[]{:S(2)}, u32[]{:S(2)}) %collective-permute-start.1) | collective-permute-done | bytes 57376 | tf_op jit(solution)/shard_map/ppermute | solution.py:26
  14.4 1.3 %shard_map.35 = (f32[2,480]{1,0:T(2,128)}, bf16[480,128]{1,0:T(8,128)(2,1)}) custom-call(bf16[480,128]{1,0:T(8,128)(2,1)S(1)} %bitcast.10, bf16[224,128]{1,0:T(8,128)(2,1)S(1)} %collective-permute-done.1.refs_1_, bf16[480,128]{1,0:T(8,128)(2,1)S(1)} %shard_map.30.refs_2_, f32[480,128]{1,0:T(8,128)S(1)} %get-tuple-element.18.refs_3_, ...), custom_call_target="tpu_custom_call" | custom-call | flops 82575360 | bytes 57344 | tf_op jit(solution)/shard_map/pallas_call | solution.py:149
  (2 shorter events, 0.0 us)
Async XLA Ops:
  0.6 7.6 %collective-permute-start = (bf16[480,128]{1,0:T(8,128)(2,1)}, bf16[480,128]{1,0:T(8,128)(2,1)S(1)}, u32[]{:S(2)}, u32[]{:S(2)}) collective-permute-start(bf16[480,128]{1,0:T(8,128)(2,1)} %bitcast.3), channel_id=1, source_target_pairs={{0,9},{1,8},{4,1},{5,0},{8,5},{9,4},{12,13},{13,12},{2,11},{3,10},... | collective-permute-start | bytes 368648 | tf_op jit(solution)/shard_map/ppermute | solution.py:26
  4.2 6.9 %collective-permute-start.4 = (bf16[480,128]{1,0:T(8,128)(2,1)}, bf16[480,128]{1,0:T(8,128)(2,1)S(1)}, u32[]{:S(2)}, u32[]{:S(2)}) collective-permute-start(bf16[480,128]{1,0:T(8,128)(2,1)} %bitcast.4), channel_id=1, source_target_pairs={{0,5},{1,4},{4,9},{5,8},{8,13},{9,12},{12,1},{13,0},{2,7},{3,6},{6... | collective-permute-start | bytes 368648 | tf_op jit(solution)/shard_map/ppermute | solution.py:26
  4.2 7.5 %collective-permute-start.3 = (bf16[480,128]{1,0:T(8,128)(2,1)}, bf16[480,128]{1,0:T(8,128)(2,1)S(1)}, u32[]{:S(2)}, u32[]{:S(2)}) collective-permute-start(bf16[480,128]{1,0:T(8,128)(2,1)} %bitcast.5), channel_id=1, source_target_pairs={{0,1},{1,0},{4,13},{5,12},{8,9},{9,8},{12,5},{13,4},{2,3},{3,2},{6... | collective-permute-start | bytes 368648 | tf_op jit(solution)/shard_map/ppermute | solution.py:26
  8.3 2.2 %copy-start = (bf16[1,1,480,128]{3,2,1,0:T(8,128)(2,1)S(1)}, bf16[1,1,480,128]{3,2,1,0:T(8,128)(2,1)}, u32[]{:S(2)}) copy-start(bf16[1,1,480,128]{3,2,1,0:T(8,128)(2,1)} %param.1) | copy-start | bytes 368644
  8.3 5.4 %collective-permute-start.2 = (bf16[256,128]{1,0:T(8,128)(2,1)S(1)}, bf16[256,128]{1,0:T(8,128)(2,1)S(1)}, u32[]{:S(2)}, u32[]{:S(2)}) collective-permute-start(bf16[256,128]{1,0:T(8,128)(2,1)S(1)} %slice.9), channel_id=1, source_target_pairs={{0,4},{1,5},{4,0},{5,1},{8,12},{9,13},{12,8},{13,9},{2,6},{3,7},{6... | collective-permute-start | bytes 196616 | tf_op jit(solution)/shard_map/ppermute | solution.py:26
  9.6 4.8 %collective-permute-start.1 = (bf16[224,128]{1,0:T(8,128)(2,1)S(1)}, bf16[224,128]{1,0:T(8,128)(2,1)S(1)}, u32[]{:S(2)}, u32[]{:S(2)}) collective-permute-start(bf16[224,128]{1,0:T(8,128)(2,1)S(1)} %slice.8), channel_id=1, source_target_pairs={{0,4},{1,5},{4,0},{5,1},{8,12},{9,13},{12,8},{13,9},{2,6},{3,7},{6... | collective-permute-start | bytes 172040 | tf_op jit(solution)/shard_map/ppermute | solution.py:26
